TPU v7x, 32 devices: a whole 2x2x4 slice. The times are simulated.
32 devices in a mesh: tm: 4 (over x, core), chan: 8 (over z, y).
Axes of the slice: x: 2, y: 2, z: 4, core: 2. Of those that a mesh axis runs over, the one named last changes fastest.
Arguments:
- raw_blocks: bfloat16 [16, 5120, 1024], P('tm', 'chan'), may hold values from -6 to 6
- fir_taps: bfloat16 [128], replicated, may hold values from -0.5 to 0.5
- recorder_channel: int32 [5120], replicated, may hold values from 0 to 5119, as said below
- pairs: int32 [4096, 2], P('chan'), may hold values from 0 to 5119, as said below
Outputs:
- stacks: float32 [4096, 256], P('chan')
Inputs may be any that keep to these rules, and one draw needn't show every extreme that they name: `recorder_channel`: A permutation of the channels; each aligned block of 640 recorder rows holds exactly 80 channels of every range of 640 consecutive channels. `pairs`: each aligned block of 512 rows names exactly 32 distinct channels of every range of 640 consecutive channels.
All inputs are finite; a program needn't handle non-finite values.
Results may differ from a plain program's by a relative error of at most 0.0084.
Values may be sent and summed in bfloat16 or wider, within the bound.
No kernel may reach another device: no remote copies, remote signals or barrier semaphores. Data moves between devices by JAX's collectives and lax.ppermute only.
A program may use at most 128 MiB of HBM per device.

v0:
```python
import jax
import jax.numpy as jnp
from jax import lax
from jax.sharding import PartitionSpec as P

NB = 128
SMOOTH = 4


def make_fir(fir_taps, length):
    taps_n = fir_taps.shape[0]
    period = taps_n + length
    padded = jnp.concatenate([fir_taps.astype(jnp.float32), jnp.zeros((length,), jnp.float32)])
    repeated = jnp.tile(padded, length)[: length * (period - 1)].reshape(length, period - 1)[
        :, :length
    ]
    return repeated.astype(jnp.bfloat16)


def make_table(length, bin_count):
    samples = jnp.arange(length, dtype=jnp.int32)
    freqs = jnp.arange(1, bin_count + 1, dtype=jnp.int32)
    phase_idx = samples[:, None] * freqs[None, :] % length
    angles = phase_idx.astype(jnp.float32) * (2.0 * jnp.pi / length)
    return jnp.concatenate([jnp.cos(angles), -jnp.sin(angles)], axis=1).astype(jnp.bfloat16)


def make_smooth(bin_count, half_width):
    places = jnp.arange(bin_count, dtype=jnp.int32)
    band_mask = (jnp.abs(places[:, None] - places[None, :]) <= half_width).astype(jnp.float32)
    return band_mask / jnp.sum(band_mask, axis=0, keepdims=True)


def whiten(spectrum, smoother):
    bin_count = spectrum.shape[-1] // 2
    real_part = spectrum[..., :bin_count]
    imag_part = spectrum[..., bin_count:]
    magnitude = jnp.sqrt(real_part * real_part + imag_part * imag_part)
    smoothed = jnp.dot(magnitude, smoother, precision=lax.Precision.HIGHEST)
    mean_level = jnp.mean(magnitude, axis=-1, keepdims=True)
    divisor = smoothed + 0.1 * mean_level + 1e-06
    return (spectrum / jnp.concatenate([divisor, divisor], axis=-1)).astype(jnp.bfloat16)


def cross(left_rows, right_rows):
    bin_count = left_rows.shape[-1] // 2
    left_f = left_rows.astype(jnp.float32)
    right_f = right_rows.astype(jnp.float32)
    left_re, left_im = (left_f[..., :bin_count], left_f[..., bin_count:])
    right_re, right_im = (right_f[..., :bin_count], right_f[..., bin_count:])
    real_out = left_re * right_re + left_im * right_im
    imag_out = left_im * right_re - left_re * right_im
    return jnp.concatenate([real_out, imag_out], axis=-1)


def local(raw_blocks, fir_taps, recorder_channel, pairs):
    windows, ch_dev, length = raw_blocks.shape
    rows_of = jnp.argsort(recorder_channel, stable=True)
    endpoints = jnp.concatenate([pairs[:, 0], pairs[:, 1]])
    wanted_ids = jnp.take(rows_of, endpoints)
    fir_matrix = make_fir(fir_taps, length)
    dft_table = make_table(length, NB)
    smoother = make_smooth(NB, SMOOTH)
    flat_rows = raw_blocks.reshape(windows * ch_dev, length)
    filtered = jnp.dot(flat_rows, fir_matrix, preferred_element_type=jnp.float32).astype(
        jnp.bfloat16
    )
    spectrum = jnp.dot(filtered, dft_table, preferred_element_type=jnp.float32)
    whitened = whiten(spectrum, smoother).reshape(windows, ch_dev, 2 * NB)
    pair_count = pairs.shape[0]
    empty = jnp.zeros((windows, 2 * pair_count, 2 * NB), jnp.bfloat16)
    part_rows = lax.all_gather(whitened, "chan", axis=1, tiled=True)
    inside = (wanted_ids >= 0) & (wanted_ids < part_rows.shape[1])
    taken = jnp.take(part_rows, jnp.clip(wanted_ids, 0, part_rows.shape[1] - 1), axis=1)
    chosen = jnp.where(inside[None, :, None], taken, empty)
    products = cross(chosen[:, :pair_count], chosen[:, pair_count:])
    stacked = jnp.sum(products, axis=0)
    summed = lax.psum(stacked, "tm")
    return summed / (windows * lax.axis_size("tm"))


def solution(mesh):
    in_specs = (P("tm", "chan", None), P(), P(), P("chan", None))
    out_specs = P("chan", None)
    return jax.shard_map(local, mesh=mesh, in_specs=in_specs, out_specs=out_specs, check_vma=False)
```

profile of v0, /device:TPU:0, one launch (start us, length us, event | category | flops | bytes accessed | tf_op | source)
XLA Modules:
  0.0 248.1 jit_solution(11060469899976761753)
XLA Ops:
  6.6 2.2 cosine_convert_fusion
  8.8 0.7 concatenate.69
  9.5 0.2 tile.10
  9.7 3.8 %tile.11 = bf16[1179648]{0:T(1024)(128)(2,1)} reshape(bf16[1024,1152]{1,0:T(8,128)(2,1)S(1)} %tile.10) | data formatting | bytes 4718592 | tf_op jit(solution)/shard_map/tile | solution.py:14
  13.5 1.7 slice-done
  15.2 6.4 %reshape.232 = bf16[1024,1151]{1,0:T(8,128)(2,1)} reshape(bf16[1178624]{0:T(1024)(128)(2,1)S(1)} %slice-done) | data formatting | bytes 4714496 | tf_op jit(solution)/shard_map/reshape | solution.py:14
  21.5 10.3 %fusion.6 = f32[2560,256]{1,0:T(8,128)S(1)} fusion(bf16[2560,1024]{1,0:T(8,128)(2,1)} %bitcast.16, bf16[1024,1151]{1,0:T(8,128)(2,1)} %reshape.232, bf16[1024,128]{1,0:T(8,128)(2,1)S(1)} %get-tuple-element.16, bf16[1024,128]{1,0:T(8,128)(2,1)S(1)} %get-tuple-element.15), kind=kOutput, calls=%fused_computation.14 | convolution fusion | flops 6714556416 | bytes 10485760 | tf_op jit(solution)/shard_map/dot_general | solution.py:68
  31.9 0.5 fusion.17
  32.4 1.5 fusion
  33.9 0.5 fusion.1
  34.5 2.1 copy.11
  36.6 0.0 all-gather.2.cloned.1.call-update
  36.6 0.0 all-reduce.3.cloned.1.call-start
  36.6 6.8 %sort.17 = (s32[5120]{0:T(1024)}, s32[5120]{0:T(1024)S(1)}) sort(s32[5120]{0:T(1024)S(1)} %copy-done, s32[5120]{0:T(1024)S(1)} %iota.22), dimensions={0}, to_apply=%region_0.0 | sort | flops 66560 | bytes 81920 | tf_op jit(solution)/shard_map/jit(argsort)/sort | solution.py:58
  43.4 6.4 %gather_fusion = s32[1024]{0:T(1024)S(1)} fusion(s32[5120]{0:T(1024)S(1)} %get-tuple-element.6, s32[1024]{0:T(1024)S(1)} %broadcast_clamp_fusion.1), kind=kCustom, calls=%fused_computation | custom fusion | bytes 12288 | tf_op jit(solution)/shard_map/jit(_take)/gather | solution.py:60
  49.9 140.1 %all-gather.2.cloned.1.call-done = bf16[4,5120,256]{2,0,1:T(4,128)(2,1)} async-done(((bf16[4,640,256]{2,0,1:T(4,128)(2,1)}), bf16[4,5120,256]{2,0,1:T(4,128)(2,1)}) %all-gather.2.cloned.1.call-update) | async-done | bytes 10485776 | tf_op jit(solution)/shard_map/all_gather | solution.py:72
  190.0 7.9 %gather_fusion.1 = bf16[1024,4,256]{2,1,0:T(4,128)(2,1)S(1)} fusion(bf16[4,5120,256]{2,0,1:T(4,128)(2,1)} %all-gather.2.cloned.1.call-done, s32[1024]{0:T(1024)S(1)} %broadcast_clamp_fusion), kind=kCustom, calls=%fused_computation.1 | custom fusion | bytes 4198400 | tf_op jit(solution)/shard_map/jit(_take)/gather | solution.py:74
  197.9 6.5 %select_bitcast_fusion = bf16[4,1024,256]{2,0,1:T(4,128)(2,1)S(1)} fusion(bf16[1024,4,256]{2,1,0:T(4,128)(2,1)S(1)} %gather_fusion.1, pred[1024]{0:T(1024)(128)(4,1)S(1)} %get-tuple-element.12, pred[1024]{0:T(1024)(128)(4,1)S(1)} %get-tuple-element.11), kind=kLoop, calls=%fused_computation.9 | loop fusion | flops 2097152 | bytes 4196352 | tf_op jit(solution)/shard_map/jit(_where)/select_n | solution.py:75
  204.4 0.5 slice_convert_fusion.1
  204.9 0.5 multiply_add_fusion
  205.5 2.2 maximum_reduce_fusion
  207.7 0.0 all-reduce.3.cloned.1.call-update
  207.7 31.7 %all-reduce.3.cloned.1.call-done = f32[512,256]{1,0:T(8,128)} async-done(((f32[512,256]{1,0:T(8,128)}), f32[512,256]{1,0:T(8,128)}) %all-reduce.3.cloned.1.call-update) | async-done | bytes 524304 | tf_op jit(solution)/shard_map/psum | solution.py:78
  239.4 1.9 broadcast_multiply_fusion
  (16 shorter events, 0.1 us)
Async XLA Ops:
  6.5 183.4 %all-gather.2.cloned.1.call-start = ((), (), s32[]{:S(2)}) async-start(), calls=%async_computation | async-start | bytes 11796480 | tf_op jit(solution)/shard_map/all_gather | solution.py:72
  13.5 1.7 slice-start
  34.4 2.2 copy-start
  34.5 9.0 %copy-start.1 = (s32[512,2]{0,1:T(2,128)S(1)}, s32[512,2]{0,1:T(2,128)}, u32[]{:S(2)}) copy-start(s32[512,2]{0,1:T(2,128)} %param.7) | copy-start | bytes 12292
  36.6 202.8 %all-reduce.3.cloned.1.call-start = ((), (), s32[]{:S(2)}) async-start(), calls=%async_computation.1 | async-start | bytes 1048576 | tf_op jit(solution)/shard_map/psum | solution.py:78
Sparse Core Ops, SparseCore 0:
  36.7 153.2 all-gather.1
  207.8 31.5 all-reduce.2
where the time goes:
time: 248 us
  waiting for transfers between devices  172 us (69%)
  local copies, waits for them, and re-layouts  29.1 us (12%)
  other arithmetic  21.8 us (9%)
  between operations  13.5 us (5%)
  matrix products  11.8 us (5%)
    all_gather x1, waiting for transfers between devices, local(): part_rows = lax.all_gather(whitened, 'chan', axis=1, tiled=True)  140 us
    psum x1, waiting for transfers between devices, local(): summed = lax.psum(stacked, 'tm')  31.7 us
    dot_general x1, matrix products, local(): spectrum = jnp.dot(filtered, dft_table, preferred_element_type=jnp.float32)  10.3 us
    gather x1, local copies, waits for them, and re-layouts, local(): jnp.take(part_rows, jnp.clip(wanted_ids, 0, part_rows.shape[1] - 1), axis=1)  7.92 us
    sort x1, other arithmetic, local(): rows_of = jnp.argsort(recorder_channel, stable=True)  6.76 us
    select_n x1, other arithmetic, local(): chosen = jnp.where(inside[None, :, None], taken, empty)  6.46 us
    gather x1, local copies, waits for them, and re-layouts, local(): wanted_ids = jnp.take(rows_of, endpoints)  6.37 us
    reshape x1, local copies, waits for them, and re-layouts, make_fir(): jnp.tile(padded, length)[:length * (period - 1)].reshape(length, period - 1)  6.35 us
  transfers between devices with their start and end apart: 2, of which 2 were waited for; matrix products, arithmetic and copies ran while one was open for 5% of the time, Pallas kernels for 0%

commit v1 on v0

v1 whole, which is shorter than its diff:
```python
import functools

import jax
import jax.numpy as jnp
import ml_dtypes
import numpy as np
from jax import lax
from jax.experimental import pallas as pl
from jax.experimental.pallas import tpu as pltpu
from jax.sharding import PartitionSpec as P

NB = 128
SMOOTH = 4
LANES = 128
MARK_FLOPS = 2 * 10**10
ROUND_ROWS = 56

F32, BF16, I32 = jnp.float32, jnp.bfloat16, jnp.int32
VMEM = pl.BlockSpec(memory_space=pltpu.VMEM)
SMEM = pl.BlockSpec(memory_space=pltpu.SMEM)
NT = (((1,), (1,)), ((), ()))


def table_of(length, pad):
    samples = np.arange(length, dtype=np.int64)
    freqs = np.arange(1, NB + 1, dtype=np.int64)
    phase = (samples[:, None] * freqs[None, :] % length).astype(np.float32)
    angles = (phase * np.float32(2.0 * np.pi / length)).astype(np.float64)
    table = np.concatenate([np.cos(angles), -np.sin(angles)], axis=1).astype(np.float32)
    table = np.concatenate([table, np.zeros((pad, 2 * NB), np.float32)])
    return table.astype(ml_dtypes.bfloat16)


def dot(a, b, dims=(((1,), (0,)), ((), ()))):
    return lax.dot_general(a, b, dims, preferred_element_type=F32)


def iota(shape, axis):
    return lax.broadcasted_iota(I32, shape, axis)


def spectrum_kernel(core_ref, taps_ref, table_ref, raw_ref, keep_ref, give_ref, rows_ref, mat_ref, sem):
    windows = raw_ref.shape[0]
    copies = [pltpu.make_async_copy(raw_ref.at[w], rows_ref.at[w], sem.at[w]) for w in range(windows)]
    for copy in copies:
        copy.start()
    taps = taps_ref[...].astype(F32)
    n = taps.shape[1]
    wide = jnp.concatenate([taps, jnp.zeros_like(taps)], axis=1)
    toeplitz = pltpu.roll(jnp.broadcast_to(wide, (n, 2 * n)), 0, 1, stride=1, stride_axis=0).astype(BF16)
    for b in range(mat_ref.shape[0] // n):
        mat_ref[b * n : (b + 1) * n, :] = dot(toeplitz, table_ref[b * n : (b + 2) * n, :]).astype(BF16)
    shape = (2 * NB, 2 * NB)
    near = jnp.abs(iota(shape, 0) % NB - iota(shape, 1)) <= SMOOTH
    averaging = jnp.where(near | (iota(shape, 1) >= NB), 1.0, 0.0).astype(BF16)
    bins = iota((1, NB), 1)
    counts = jnp.minimum(bins, SMOOTH) + jnp.minimum(NB - 1 - bins, SMOOTH) + 1
    inverse = 1.0 / counts.astype(F32)
    first_core = core_ref[0] == 0
    half = NB // 2

    def whiten(w, spec):
        re, im = spec[:, :NB], spec[:, NB:]
        mag = jnp.sqrt(re * re + im * im)
        high = mag.astype(BF16)
        low = (mag - high.astype(F32)).astype(BF16)
        sums = dot(jnp.concatenate([high, low], axis=1), averaging)
        divisor = sums[:, :NB] * inverse + sums[:, NB:] * (0.1 / NB) + 1e-06
        scale = 1.0 / divisor
        re = re * scale
        im = im * scale
        left = iota(re.shape, 1) < half
        first = jnp.where(left, re, pltpu.roll(im, half, 1))
        second = jnp.where(left, pltpu.roll(re, half, 1), im)
        keep_ref[w] = jnp.where(first_core, first, second).astype(BF16)
        give_ref[w] = jnp.where(first_core, second, first).astype(BF16)

    for start in range(0, windows, 2):
        pair = range(start, min(start + 2, windows))
        for w in pair:
            copies[w].wait()
        specs = [dot(rows_ref[w], mat_ref[...]) for w in pair]
        for w, spec in zip(pair, specs):
            whiten(w, spec)


def lane_sum(value):
    return jnp.sum(value, axis=1, keepdims=True)


def mark_kernel(high_count, pairs_ref, marks_ref):
    table = None
    for j in range(2):
        ids = pairs_ref[j : j + 1, :]
        high = (iota((high_count, ids.shape[1]), 0) == ids // LANES).astype(F32).astype(BF16)
        low = (iota((LANES, ids.shape[1]), 0) == ids % LANES).astype(F32).astype(BF16)
        part = dot(high, low, NT)
        table = part if table is None else table + part
    bits = jnp.where(table > 0.5, 1, 0) << (iota(table.shape, 0) % 32)
    for w in range(marks_ref.shape[1] // LANES):
        word = bits[32 * w : min(32 * w + 32, high_count), :]
        marks_ref[:, w * LANES : (w + 1) * LANES] = jnp.sum(word, axis=0, keepdims=True)


def wanted(marks, ids):
    parts = []
    words = marks.shape[1] // LANES
    for g in range(ids.shape[1] // LANES):
        here = ids[:, g * LANES : (g + 1) * LANES]
        high, low = here // LANES, here % LANES
        found = jnp.zeros_like(here)
        for w in range(words):
            word = jnp.take_along_axis(marks[:, w * LANES : (w + 1) * LANES], low, axis=1)
            found = jnp.where(high // 32 == w, word, found)
        parts.append((found >> (high % 32)) & 1)
    return parts


def places(parts):
    ahead = (iota((LANES, LANES), 0) < iota((LANES, LANES), 1)).astype(F32).astype(BF16)
    count = None
    out = []
    for part in parts:
        value = part.astype(F32)
        place = dot(value.astype(BF16), ahead)
        if count is not None:
            place = place + count
        out.append(jnp.where(part > 0, place, -1.0).astype(I32))
        total = lane_sum(value)
        count = total if count is None else count + total
    return jnp.concatenate(out, axis=1), count


def spread(row, count):
    return jnp.broadcast_to(row, (count, row.shape[1]))


def stacked(refs):
    marks = jnp.concatenate([ref[...] for ref in refs], axis=0)
    pad = -marks.shape[0] % 8
    if pad:
        marks = jnp.concatenate([marks, jnp.zeros((pad, marks.shape[1]), I32)], axis=0)
    return marks


def pack_kernel(lines, pieces, me_ref, *refs):
    marks = stacked(refs[:pieces])
    chan_ref, keep_ref, other_ref = refs[pieces : pieces + 3]
    chunk_refs = refs[pieces + 3 :]
    chunk = chunk_refs[0].shape[0]
    rows = chan_ref.shape[1]
    ids = spread(chan_ref[pl.ds(me_ref[0], 1), :], marks.shape[0])
    place, _ = places(wanted(marks, ids))
    slots = iota((chunk, rows), 0)
    select = [(slots == place[i : i + 1, :]).astype(F32).astype(BF16) for i in lines]
    select = jnp.concatenate(select, axis=0)
    for w in range(keep_ref.shape[0]):
        data = jnp.concatenate([keep_ref[w], other_ref[w]], axis=1)
        out = dot(select, data).astype(BF16)
        for i in range(len(lines)):
            chunk_refs[i][:, 2 * w * LANES : 2 * (w + 1) * LANES] = out[i * chunk : (i + 1) * chunk]


def arrival_kernel(sources, chunk, pieces, me_ref, *refs):
    marks = stacked(refs[:pieces])
    chan_ref, pairs_ref, early_ref, late_ref, most_ref = refs[pieces:]
    n = len(sources)
    ids = jnp.concatenate([chan_ref[pl.ds(me_ref[0] ^ k, 1), :] for k in sources], axis=0)
    most = None
    for k in range(n):
        parts = wanted(spread(marks[k : k + 1, :], n), ids)
        if k == 0:
            place, count = places(parts)
        else:
            count = lane_sum(sum(parts).astype(F32))
        most = count if most is None else jnp.maximum(most, count)
    most_ref[...] = jnp.max(most, axis=0, keepdims=True).astype(I32)
    slots = iota((chunk, ids.shape[1]), 0)
    here = []
    for s in range(n):
        held = jnp.where(slots == place[s : s + 1, :], ids[s : s + 1, :] + 1, 0)
        here.append(lane_sum(held.astype(F32)))
    column = jnp.concatenate(here, axis=0) - 1.0
    row = jnp.broadcast_to(column, (n * chunk, LANES)).T[:1, :]
    ends = pairs_ref[...].astype(F32)
    count = ends.shape[1]
    ends = jnp.concatenate([ends, jnp.zeros((6, count), F32)], axis=0).T
    middle = n // 2 * chunk
    for j in range(2):
        match = ends[:, j : j + 1] == row
        match = jnp.where(match, 1.0, 0.0).astype(BF16)
        early_ref[j * count : (j + 1) * count, :] = match[:, :middle]
        late_ref[j * count : (j + 1) * count, :] = match[:, middle:]


def early_kernel(half, gather_ref, *refs):
    chunk_refs, out_ref, rows_ref = refs[:half], refs[half], refs[half + 1]
    chunk = chunk_refs[0].shape[0]
    for k in range(half):
        rows_ref[k * chunk : (k + 1) * chunk, :] = chunk_refs[k][...]
    for w in range(0, rows_ref.shape[1], 2 * LANES):
        out_ref[:, w : w + 2 * LANES] = dot(gather_ref[...], rows_ref[:, w : w + 2 * LANES]).astype(BF16)


def product_kernel(half, start, early_ref, gather_ref, *refs):
    chunk_refs, out_ref, rows_ref = refs[:half], refs[half], refs[half + 1]
    chunk = chunk_refs[0].shape[0]
    for k in range(half):
        rows_ref[k * chunk : (k + 1) * chunk, :] = chunk_refs[k][...]
    count = out_ref.shape[0]
    total = gather_ref.shape[0] // 2
    pick = jnp.concatenate([gather_ref[start : start + count, :], gather_ref[total + start : total + start + count, :]])
    middle = LANES // 2
    straight = crossed = None
    for w in range(0, rows_ref.shape[1] // LANES, 2):
        ends = dot(pick, rows_ref[:, w * LANES : (w + 2) * LANES])
        for v in range(2):
            lanes = slice((w + v) * LANES, (w + v + 1) * LANES)
            a = ends[:count, v * LANES : (v + 1) * LANES] + early_ref[start : start + count, lanes].astype(F32)
            b = ends[count:, v * LANES : (v + 1) * LANES] + early_ref[total + start : total + start + count, lanes].astype(F32)
            turned = pltpu.roll(a, middle, 1)
            straight = a * b if straight is None else straight + a * b
            crossed = turned * b if crossed is None else crossed + turned * b
    real = straight + pltpu.roll(straight, middle, 1)
    imag = pltpu.roll(crossed, middle, 1) - crossed
    out_ref[...] = jnp.where(iota(real.shape, 1) < middle, real, imag).astype(out_ref.dtype)


def finish_kernel(factor, core_ref, *refs):
    parts = (len(refs) - 1) // 2
    out_ref = refs[-1]
    first_core = core_ref[0] == 0
    half = LANES // 2
    start = 0
    for i in range(parts):
        mine = refs[i][...] * factor
        other = refs[parts + i][...] * factor
        first = jnp.where(first_core, mine, other)
        second = jnp.where(first_core, other, mine)
        left = iota(first.shape, 1) < half
        here = slice(start, start + first.shape[0])
        start += first.shape[0]
        out_ref[here, :LANES] = jnp.where(left, first, pltpu.roll(second, half, 1))
        out_ref[here, LANES:] = jnp.where(left, pltpu.roll(first, half, 1), second)


def swap(value, axis, size, bit):
    return lax.ppermute(value, axis, [(i, i ^ bit) for i in range(size)])


def call(kernel, out, flops=0, scratch=(), smem=1):
    def run(*args):
        many = isinstance(out, (tuple, list))
        specs = [SMEM] * smem + [VMEM] * (len(args) - smem)
        outs = list(out) if many else [out]
        size = sum(a.size * a.dtype.itemsize for a in args) + sum(o.size * o.dtype.itemsize for o in outs)
        return pl.pallas_call(
            kernel,
            out_shape=tuple(out) if many else out,
            in_specs=specs,
            out_specs=(VMEM,) * len(outs) if many else VMEM,
            scratch_shapes=scratch,
            compiler_params=pltpu.CompilerParams(vmem_limit_bytes=24 * 1024 * 1024),
            cost_estimate=pl.CostEstimate(flops=flops, bytes_accessed=size, transcendentals=0),
        )(*args)

    return run


def spectra(tm, core, raw_blocks, fir_taps):
    windows, rows, length = raw_blocks.shape
    table = jnp.asarray(table_of(length, fir_taps.shape[0]))
    half = jax.ShapeDtypeStruct((windows, rows, NB), BF16)
    keep, give = pl.pallas_call(
        spectrum_kernel,
        out_shape=(half, half),
        in_specs=[SMEM, VMEM, VMEM, pl.BlockSpec(memory_space=pl.ANY)],
        out_specs=(VMEM, VMEM),
        scratch_shapes=[
            pltpu.VMEM(raw_blocks.shape, BF16),
            pltpu.VMEM((length, 2 * NB), BF16),
            pltpu.SemaphoreType.DMA((windows,)),
        ],
        compiler_params=pltpu.CompilerParams(vmem_limit_bytes=24 * 1024 * 1024),
        cost_estimate=pl.CostEstimate(
            flops=2 * windows * rows * length * 2 * NB, bytes_accessed=2 * windows * rows * length, transcendentals=0
        ),
    )(core, fir_taps.reshape(1, -1), table, raw_blocks)
    return keep, swap(give, "tm", tm, 1)


def all_rounds(tm, n, chunk, order, me, core, raw_blocks, fir_taps, by_block, pairs, marks, most):
    windows, rows, _ = raw_blocks.shape
    pair_count = pairs.shape[0]
    width = 2 * windows * LANES
    data = jnp.concatenate(spectra(tm, core, raw_blocks, fir_taps), axis=0)
    data = data.transpose(1, 0, 2).reshape(rows, width)
    marks = jnp.concatenate(marks)

    def is_marked(words, ids):
        word = words.reshape(-1)[(ids // LANES // 32) * LANES + ids % LANES]
        return (word >> (ids // LANES % 32)) & 1

    mine = by_block[me[0]]
    want = jnp.stack([is_marked(marks[order.index(k)], mine) for k in range(n)])
    place = jnp.where(want > 0, jnp.cumsum(want, axis=1) - 1, -1)
    held = is_marked(marks[0], by_block)
    rank = jnp.cumsum(held, axis=1) - 1
    relative = jnp.arange(n, dtype=I32) ^ me[0]
    counts = jnp.sum(held, axis=1)[relative]
    offsets = jnp.cumsum(counts) - counts
    line_of_row = (offsets[relative][:, None] + rank).reshape(-1)
    ends = pairs.T.reshape(-1)
    line = jnp.sum(jnp.where(ends[:, None] == by_block.reshape(1, -1), line_of_row[None, :], 0), axis=1)
    lines = jnp.arange(n * chunk, dtype=I32)

    def again(inner):
        done, merged = inner
        slot = jnp.arange(chunk, dtype=I32) + done
        select = (slot[None, :, None] == place[:, None, :]).astype(BF16).reshape(n * chunk, rows)
        packed = dot(select, data).astype(BF16)
        new = [packed[k * chunk : (k + 1) * chunk] for k in range(n)]
        new = jnp.concatenate([swap(new[k], "chan", n, k) if k else new[k] for k in range(n)])
        target = jnp.where(slot[None, :] < counts[:, None], offsets[:, None] + slot[None, :], -1).reshape(1, -1)
        return done + chunk, merged + dot((lines[:, None] == target).astype(BF16), new).astype(BF16)

    start = (jnp.int32(0), jnp.zeros((n * chunk, width), BF16))
    _, merged = lax.while_loop(lambda inner: inner[0] < most[0, 0], again, start)
    taken = dot((lines[None, :] == line[:, None]).astype(BF16), merged)
    taken = taken.reshape(2, pair_count, 2 * windows, 2, LANES // 2)
    a, b = taken[0], taken[1]
    real = jnp.sum(a[:, :, 0] * b[:, :, 0] + a[:, :, 1] * b[:, :, 1], axis=1)
    imag = jnp.sum(a[:, :, 1] * b[:, :, 0] - a[:, :, 0] * b[:, :, 1], axis=1)
    total = jnp.concatenate([real, imag], axis=1)
    bit = 2
    while bit < tm:
        total = total + swap(total, "tm", tm, bit)
        bit *= 2
    return finish(core, tm, windows, [total], [swap(total, "tm", tm, 1)])


def finish(core, tm, windows, mine, other):
    rows = sum(value.shape[0] for value in mine)
    kernel = functools.partial(finish_kernel, 1.0 / (windows * tm))
    return call(kernel, jax.ShapeDtypeStruct((rows, 2 * LANES), F32))(core, *mine, *other)


def steps_of(n):
    bits = [n // 2] + [1 << i for i in range(n.bit_length() - 2)]
    order, known = [0], []
    for bit in bits:
        known.append([k ^ bit for k in order])
        order = order + known[-1]
    return bits, known, order


def arrivals(n):
    _, known, _ = steps_of(n)
    sends = [k for ks in known for k in sorted(ks) if k >= n // 2] + list(range(n // 2 - 1, 0, -1))
    return sends, [0] + sends[: n // 2 - 1], sends[n // 2 - 1 :]


def local(tm, n, raw_blocks, fir_taps, recorder_channel, pairs):
    windows, rows, _ = raw_blocks.shape
    pair_count = pairs.shape[0]
    chunk = ROUND_ROWS
    half = n // 2
    high_count = n * rows // LANES
    shaped = jax.ShapeDtypeStruct
    me = lax.axis_index("chan").astype(I32).reshape(1)
    core = (lax.axis_index("tm") % 2).astype(I32).reshape(1)
    by_block = recorder_channel.reshape(n, rows)
    width = 2 * windows * LANES
    bits, known, order = steps_of(n)
    _, early, late = arrivals(n)

    mark_shape = shaped((1, -(-high_count // 32) * LANES), I32)
    own = call(functools.partial(mark_kernel, high_count), mark_shape, flops=MARK_FLOPS, smem=0)(pairs.T)
    keep, other = spectra(tm, core, raw_blocks, fir_taps)

    marks = [own]
    arrived = [None] * n
    for i, bit in enumerate(bits):
        new = swap(jnp.concatenate(marks), "chan", n, bit)
        here = [new] if i else [new, own]
        marks.append(new)
        owners = known[i] if i else known[i] + [0]
        kernel = functools.partial(pack_kernel, list(range(len(owners))), len(here))
        packed = call(kernel, [shaped((chunk, width), BF16)] * len(owners))(me, *here, by_block, keep, other)
        for k, value in zip(owners, packed):
            arrived[k] = swap(value, "chan", n, k) if k else value

    shapes = [shaped((2 * pair_count, half * chunk), BF16)] * 2 + [shaped((1, 1), I32)]
    kernel = functools.partial(arrival_kernel, early + late, chunk, len(marks))
    pick_early, pick_late, most = call(kernel, shapes)(me, *marks, by_block, pairs.T)
    scratch = [pltpu.VMEM((half * chunk, width), BF16)]
    found = call(
        functools.partial(early_kernel, half),
        shaped((2 * pair_count, width), BF16),
        flops=4 * pair_count * half * chunk * width,
        scratch=scratch,
        smem=0,
    )(pick_early, *[arrived[k] for k in early])

    sizes = [pair_count * 3 // 4, pair_count // 4]
    totals, seconds = [], []
    for i, size in enumerate(sizes):
        total = call(
            functools.partial(product_kernel, half, sum(sizes[:i])),
            shaped((size, LANES), BF16),
            flops=4 * size * half * chunk * width,
            scratch=scratch,
            smem=0,
        )(found, pick_late, *[arrived[k] for k in late])
        bit = 2
        while bit < tm:
            sent = total.astype(BF16)
            total = sent.astype(F32) + swap(sent, "tm", tm, bit).astype(F32)
            bit *= 2
        totals.append(total.astype(F32))
    for total in totals:
        seconds.append(swap(total, "tm", tm, 1))
    result = finish(core, tm, windows, totals, seconds)

    def rounds(state):
        given = lax.optimization_barrier((state[0], me, core, raw_blocks, fir_taps, by_block, pairs, marks, most))
        return jnp.int32(0), all_rounds(tm, n, chunk, order, *given[1:])

    more = jnp.where(most[0, 0] > chunk, 1, 0)
    return lax.while_loop(lambda state: state[0] > 0, rounds, (more, result))[1]


def solution(mesh):
    tm, n = mesh.shape["tm"], mesh.shape["chan"]
    in_specs = (P("tm", "chan", None), P(), P(), P("chan", None))
    out_specs = P("chan", None)

    def body(*args):
        return local(tm, n, *args)

    return jax.shard_map(body, mesh=mesh, in_specs=in_specs, out_specs=out_specs, check_vma=False)
```

time: 248 us -> 49.2 us (0.20)
  waiting for transfers between devices: 172 us -> 15 us
  local copies, waits for them, and re-layouts: 29.1 us -> 1.08 us
  other arithmetic: 21.8 us -> 0.05 us
  starting transfers between devices: 0.04 us -> 20.4 us
  between operations: 13.5 us -> 0.81 us
  matrix products: 11.8 us -> 0 us
  Pallas kernels: 0 us -> 11.7 us
    all_gather x1 -> x0, waiting for transfers between devices: 140 us -> none  [local(): part_rows = lax.all_gather(whitened, 'chan', axis=1, tiled=True)]
    psum x1 -> x0, waiting for transfers between devices: 31.7 us -> none  [local(): summed = lax.psum(stacked, 'tm')]
    ppermute x0 -> x15, starting transfers between devices: none -> 20.4 us  [swap(): return lax.ppermute(value, axis, [(i, i ^ bit) for i in range(size)])]
    ppermute x0 -> x15, waiting for transfers between devices: none -> 15 us  [swap(): return lax.ppermute(value, axis, [(i, i ^ bit) for i in range(size)])]
    gather x2 -> x0, local copies, waits for them, and re-layouts: 14.3 us -> none  [the longest x1 7.92 us: local(): jnp.take(part_rows, jnp.clip(wanted_ids, 0, part_rows.shape[1] - 1), axis=1)]
    dot_general x2 -> x0, matrix products: 11.8 us -> none  [the longest x1 10.3 us: local(): spectrum = jnp.dot(filtered, dft_table, preferred_element_type=jnp.float32)]
    pallas_call x0 -> x10, Pallas kernels: none -> 11.7 us  [the longest x9 6.55 us: run(): pl.pallas_call(kernel, out_shape=tuple(out) if many else out, in_specs=sp...]
    reshape x2 -> x1, local copies, waits for them, and re-layouts: 8.44 us -> 0.01 us  [local(): by_block = recorder_channel.reshape(n, rows)]
  transfers between devices with their start and end apart: 2 -> 15, of which waited for: 2 -> 10; matrix products, arithmetic and copies ran while one was open for 5% -> 0% of each run, Pallas kernels for 0% -> 8%
where the time goes in v1:
time: 49.2 us; the launch traced here: 49 us
  starting transfers between devices  20.4 us (41%)
  waiting for transfers between devices  15 us (30%)
  Pallas kernels  11.7 us (24%)
  local copies, waits for them, and re-layouts  1.08 us (2%)
  between operations  0.81 us (2%)
    ppermute x15, starting transfers between devices, swap(): return lax.ppermute(value, axis, [(i, i ^ bit) for i in range(size)])  20.4 us
    ppermute x15, waiting for transfers between devices, swap(): return lax.ppermute(value, axis, [(i, i ^ bit) for i in range(size)])  15 us
    pallas_call x9, Pallas kernels, run(): pl.pallas_call(kernel, out_shape=tuple(out) if many else out, in_specs=sp...  6.55 us
    pallas_call x1, Pallas kernels, spectra(): pl.pallas_call(spectrum_kernel, out_shape=(half, half), in_specs=[SMEM, V...  5.2 us
    unnamed x8, local copies, waits for them, and re-layouts  1.08 us
  transfers between devices with their start and end apart: 15, of which 10 were waited for; matrix products, arithmetic and copies ran while one was open for 0% of the time, Pallas kernels for 8%

profile of v1, /device:TPU:0, one launch (start us, length us, event | category | flops | bytes accessed | tf_op | source)
XLA Modules:
  0.0 49.0 jit_solution(17973865482091849413)
XLA Ops:
  0.0 1.1 %copy-done.1 = bf16[1152,256]{1,0:T(8,128)(2,1)S(1)} copy-done((bf16[1152,256]{1,0:T(8,128)(2,1)S(1)}, bf16[1152,256]{1,0:T(8,128)(2,1)}, u32[]{:S(2)}) %copy-start.1) | copy-done | bytes 589848
  1.1 5.2 %shard_map.66 = (bf16[4,640,128]{2,1,0:T(8,128)(2,1)S(1)}, bf16[4,640,128]{2,1,0:T(8,128)(2,1)S(1)}) custom-call(s32[1]{0:T(128)} %bitcast.3.core_ref, bf16[1,128]{1,0:T(2,128)(2,1)} %bitcast.104, bf16[1152,256]{1,0:T(8,128)(2,1)S(1)} %copy-done.1, bf16[4,640,1024]{2,1,0:T(8,128)(2,1)} %raw_ref.1), custom_call_target="tpu_custom_call" | custom-call | flops 1342177280 | bytes 5242880 | tf_op jit(solution)/shard_map/pallas_call | solution.py:274
  6.3 0.6 %collective-permute-start.13 = (bf16[4,640,128]{2,1,0:T(8,128)(2,1)S(1)}, bf16[4,640,128]{2,1,0:T(8,128)(2,1)S(1)}, u32[]{:S(2)}, u32[]{:S(2)}) collective-permute-start(bf16[4,640,128]{2,1,0:T(8,128)(2,1)S(1)} %get-tuple-element.147), channel_id=1, source_target_pairs={{0,8},{8,0},{16,24},{24,16},{1,9},{9,1},{17,25},{25,17},{2,10},{10... | collective-permute-start | bytes 1966088 | tf_op jit(solution)/shard_map/ppermute | solution.py:248
  7.1 3.7 %collective-permute-start.10 = (s32[1,256]{1,0:T(1,128)S(1)}, s32[1,256]{1,0:T(1,128)S(1)}, u32[]{:S(2)}, u32[]{:S(2)}) collective-permute-start(s32[1,256]{1,0:T(1,128)S(1)} %shard_map.64.refs_0_.refs_1_), channel_id=1, source_target_pairs={{0,4},{1,5},{2,6},{3,7},{4,0},{5,1},{6,2},{7,3},{8,12},{9,13},{10,... | collective-permute-start | bytes 3080 | tf_op jit(solution)/shard_map/ppermute | solution.py:248
  10.7 1.6 %collective-permute-done.10.refs_1_.refs_0_ = s32[1,256]{1,0:T(1,128)S(1)} collective-permute-done((s32[1,256]{1,0:T(1,128)S(1)}, s32[1,256]{1,0:T(1,128)S(1)}, u32[]{:S(2)}, u32[]{:S(2)}) %collective-permute-start.10) | collective-permute-done | bytes 1056 | tf_op jit(solution)/shard_map/ppermute | solution.py:248
  12.3 1.9 %collective-permute-start.11 = (s32[2,256]{1,0:T(2,128)S(1)}, s32[2,256]{1,0:T(2,128)S(1)}, u32[]{:S(2)}, u32[]{:S(2)}) collective-permute-start(s32[2,256]{1,0:T(2,128)S(1)} %pad_add_fusion.1), channel_id=1, source_target_pairs={{0,1},{1,0},{2,3},{3,2},{4,5},{5,4},{6,7},{7,6},{8,9},{9,8},{10,11... | collective-permute-start | bytes 6152 | tf_op jit(solution)/shard_map/ppermute | solution.py:248
  14.2 1.7 %collective-permute-done.11.refs_2_.refs_0_ = s32[2,256]{1,0:T(2,128)S(1)} collective-permute-done((s32[2,256]{1,0:T(2,128)S(1)}, s32[2,256]{1,0:T(2,128)S(1)}, u32[]{:S(2)}, u32[]{:S(2)}) %collective-permute-start.11) | collective-permute-done | bytes 2080 | tf_op jit(solution)/shard_map/ppermute | solution.py:248
  16.4 3.9 %collective-permute-start.15 = (bf16[56,1024]{1,0:T(8,128)(2,1)S(1)}, bf16[56,1024]{1,0:T(8,128)(2,1)S(1)}, u32[]{:S(2)}, u32[]{:S(2)}) collective-permute-start(bf16[56,1024]{1,0:T(8,128)(2,1)S(1)} %get-tuple-element.150), channel_id=1, source_target_pairs={{0,5},{1,4},{2,7},{3,6},{4,1},{5,0},{6,3},{7,2},{8,13},{9,12},{10,... | collective-permute-start | bytes 344072 | tf_op jit(solution)/shard_map/ppermute | solution.py:248
  21.3 1.6 %collective-permute-start.12 = (s32[4,256]{1,0:T(4,128)S(1)}, s32[4,256]{1,0:T(4,128)S(1)}, u32[]{:S(2)}, u32[]{:S(2)}) collective-permute-start(s32[4,256]{1,0:T(4,128)S(1)} %pad_add_fusion), channel_id=1, source_target_pairs={{0,2},{1,3},{2,0},{3,1},{4,6},{5,7},{6,4},{7,5},{8,10},{9,11},{10,... | collective-permute-start | bytes 12296 | tf_op jit(solution)/shard_map/ppermute | solution.py:248
  22.9 2.0 %collective-permute-done.12.refs_3_.refs_0_ = s32[4,256]{1,0:T(4,128)S(1)} collective-permute-done((s32[4,256]{1,0:T(4,128)S(1)}, s32[4,256]{1,0:T(4,128)S(1)}, u32[]{:S(2)}, u32[]{:S(2)}) %collective-permute-start.12) | collective-permute-done | bytes 4128 | tf_op jit(solution)/shard_map/ppermute | solution.py:248
  24.9 0.7 %shard_map.69 = (bf16[56,1024]{1,0:T(8,128)(2,1)S(1)}, bf16[56,1024]{1,0:T(8,128)(2,1)S(1)}, bf16[56,1024]{1,0:T(8,128)(2,1)S(1)}, bf16[56,1024]{1,0:T(8,128)(2,1)S(1)}) custom-call(s32[1]{0:T(128)} %bitcast.me_ref, s32[4,256]{1,0:T(4,128)S(1)} %collective-permute-done.12.refs_3_.refs_0_, s32[8,640]{1,0:T(8,128)S(1)} %reshape.337.refs_4_.refs_2_.refs_1_, ...), custom_call_target="tpu_custom_call" | custom-call | bytes 1794052 | tf_op jit(solution)/shard_map/pallas_call | solution.py:257
  25.7 4.1 %collective-permute-start.16 = (bf16[56,1024]{1,0:T(8,128)(2,1)S(1)}, bf16[56,1024]{1,0:T(8,128)(2,1)S(1)}, u32[]{:S(2)}, u32[]{:S(2)}) collective-permute-start(bf16[56,1024]{1,0:T(8,128)(2,1)S(1)} %get-tuple-element.151), channel_id=1, source_target_pairs={{0,6},{1,7},{2,4},{3,5},{4,2},{5,3},{6,0},{7,1},{8,14},{9,15},{10,... | collective-permute-start | bytes 344072 | tf_op jit(solution)/shard_map/ppermute | solution.py:248
  30.2 1.0 %collective-permute-start.17 = (bf16[56,1024]{1,0:T(8,128)(2,1)S(1)}, bf16[56,1024]{1,0:T(8,128)(2,1)S(1)}, u32[]{:S(2)}, u32[]{:S(2)}) collective-permute-start(bf16[56,1024]{1,0:T(8,128)(2,1)S(1)} %get-tuple-element.153), channel_id=1, source_target_pairs={{0,7},{1,6},{2,5},{3,4},{4,3},{5,2},{6,1},{7,0},{8,15},{9,14},{10,... | collective-permute-start | bytes 344072 | tf_op jit(solution)/shard_map/ppermute | solution.py:248
  31.7 2.6 %collective-permute-done.14.refs_1_ = bf16[56,1024]{1,0:T(8,128)(2,1)S(1)} collective-permute-done((bf16[56,1024]{1,0:T(8,128)(2,1)S(1)}, bf16[56,1024]{1,0:T(8,128)(2,1)S(1)}, u32[]{:S(2)}, u32[]{:S(2)}) %collective-permute-start.14) | collective-permute-done | bytes 114720 | tf_op jit(solution)/shard_map/ppermute | solution.py:248
  34.4 1.4 %shard_map.65 = (bf16[1024,224]{1,0:T(8,128)(2,1)S(1)}, bf16[1024,224]{1,0:T(8,128)(2,1)S(1)}, s32[1,1]{1,0:T(1,128)}) custom-call(s32[1]{0:T(128)} %bitcast.me_ref, s32[1,256]{1,0:T(1,128)S(1)} %shard_map.64.refs_0_.refs_1_, s32[1,256]{1,0:T(1,128)S(1)} %collective-permute-done.10.refs_1_.refs_0_, s32[2,256]{1,0:T(2,128)S(1)} %collective-permute-done.11.refs_2_.refs_0_, ...), custom_call_target="tpu_custom_call" | custom-call | bytes 950280 | tf_op jit(solution)/shard_map/pallas_call | solution.py:257
  35.8 0.7 %shard_map.70.early_ref = bf16[1024,1024]{1,0:T(8,128)(2,1)S(1)} custom-call(bf16[1024,224]{1,0:T(8,128)(2,1)S(1)} %get-tuple-element.145.gather_ref, bf16[56,1024]{1,0:T(8,128)(2,1)S(1)} %get-tuple-element.148.refs_0_, bf16[56,1024]{1,0:T(8,128)(2,1)S(1)} %collective-permute-done.14.refs_1_, bf16[56,1024]{1,0:T(8,128)(2,1)S(1)} %collective-permute-done.15.refs_2_, ...), custom_call_target="tpu_custom_call" | custom-call | flops 469762048 | bytes 3014656 | tf_op jit(solution)/shard_map/pallas_call | solution.py:257
  36.5 1.9 %collective-permute-done.17.refs_0_ = bf16[56,1024]{1,0:T(8,128)(2,1)S(1)} collective-permute-done((bf16[56,1024]{1,0:T(8,128)(2,1)S(1)}, bf16[56,1024]{1,0:T(8,128)(2,1)S(1)}, u32[]{:S(2)}, u32[]{:S(2)}) %collective-permute-start.17) | collective-permute-done | bytes 114720 | tf_op jit(solution)/shard_map/ppermute | solution.py:248
  38.5 1.3 %collective-permute-done.19.refs_2_ = bf16[56,1024]{1,0:T(8,128)(2,1)S(1)} collective-permute-done((bf16[56,1024]{1,0:T(8,128)(2,1)S(1)}, bf16[56,1024]{1,0:T(8,128)(2,1)S(1)}, u32[]{:S(2)}, u32[]{:S(2)}) %collective-permute-start.19) | collective-permute-done | bytes 114720 | tf_op jit(solution)/shard_map/ppermute | solution.py:248
  39.7 1.0 %shard_map.71 = bf16[384,128]{1,0:T(8,128)(2,1)S(1)} custom-call(bf16[1024,1024]{1,0:T(8,128)(2,1)S(1)} %shard_map.70.early_ref, bf16[1024,224]{1,0:T(8,128)(2,1)S(1)} %get-tuple-element.152.gather_ref, bf16[56,1024]{1,0:T(8,128)(2,1)S(1)} %collective-permute-done.17.refs_0_, bf16[56,1024]{1,0:T(8,128)(2,1)S(1)} %collective-permute-done.18.refs_1_, ...), custom_call_target="tpu_custom_call" | custom-call | flops 352321536 | bytes 3112960 | tf_op jit(solution)/shard_map/pallas_call | solution.py:257
  40.7 1.5 %collective-permute-start.21 = (bf16[384,128]{1,0:T(8,128)(2,1)S(1)}, bf16[384,128]{1,0:T(8,128)(2,1)S(1)}, u32[]{:S(2)}, u32[]{:S(2)}) collective-permute-start(bf16[384,128]{1,0:T(8,128)(2,1)S(1)} %shard_map.71), channel_id=1, source_target_pairs={{0,16},{8,24},{16,0},{24,8},{1,17},{9,25},{17,1},{25,9},{2,18},{10... | collective-permute-start | bytes 294920 | tf_op jit(solution)/shard_map/ppermute | solution.py:248
  42.7 0.6 %collective-permute-start.22 = (bf16[128,128]{1,0:T(8,128)(2,1)S(1)}, bf16[128,128]{1,0:T(8,128)(2,1)S(1)}, u32[]{:S(2)}, u32[]{:S(2)}) collective-permute-start(bf16[128,128]{1,0:T(8,128)(2,1)S(1)} %shard_map.72), channel_id=1, source_target_pairs={{0,16},{8,24},{16,0},{24,8},{1,17},{9,25},{17,1},{25,9},{2,18},{10... | collective-permute-start | bytes 98312 | tf_op jit(solution)/shard_map/ppermute | solution.py:248
  43.3 2.1 %collective-permute-done.21 = bf16[384,128]{1,0:T(8,128)(2,1)S(1)} collective-permute-done((bf16[384,128]{1,0:T(8,128)(2,1)S(1)}, bf16[384,128]{1,0:T(8,128)(2,1)S(1)}, u32[]{:S(2)}, u32[]{:S(2)}) %collective-permute-start.21) | collective-permute-done | bytes 98336 | tf_op jit(solution)/shard_map/ppermute | solution.py:248
  45.5 1.2 %collective-permute-done.22 = bf16[128,128]{1,0:T(8,128)(2,1)S(1)} collective-permute-done((bf16[128,128]{1,0:T(8,128)(2,1)S(1)}, bf16[128,128]{1,0:T(8,128)(2,1)S(1)}, u32[]{:S(2)}, u32[]{:S(2)}) %collective-permute-start.22) | collective-permute-done | bytes 32800 | tf_op jit(solution)/shard_map/ppermute | solution.py:248
  48.0 1.0 %shard_map.73 = f32[512,256]{1,0:T(8,128)} custom-call(s32[1]{0:T(128)} %bitcast.3.core_ref, f32[384,128]{1,0:T(8,128)S(1)} %convert_add_fusion.refs_0_, f32[128,128]{1,0:T(8,128)S(1)} %convert_add_fusion.1.refs_1_, f32[384,128]{1,0:T(8,128)S(1)} %collective-permute-done.23.refs_2_, f32[128,128]{1,0:T(8,128)S(1)} %collective-permute-done.24.refs_3_), custom_call_target="tpu_custom_call" | custom-call | bytes 1048580 | tf_op jit(solution)/shard_map/pallas_call | solution.py:257
  (30 shorter events, 4.0 us)
Async XLA Ops:
  0.0 1.1 %copy-start.1 = (bf16[1152,256]{1,0:T(8,128)(2,1)S(1)}, bf16[1152,256]{1,0:T(8,128)(2,1)}, u32[]{:S(2)}) copy-start(bf16[1152,256]{1,0:T(8,128)(2,1)} %constant.231.clone.table_ref) | copy-start | bytes 1769476
  1.1 5.8 %copy-start.2 = (s32[512,2]{0,1:T(2,128)S(1)}, s32[512,2]{0,1:T(2,128)}, u32[]{:S(2)}) copy-start(s32[512,2]{0,1:T(2,128)} %param.13) | copy-start | bytes 12292
  6.3 9.6 %collective-permute-start.13 = (bf16[4,640,128]{2,1,0:T(8,128)(2,1)S(1)}, bf16[4,640,128]{2,1,0:T(8,128)(2,1)S(1)}, u32[]{:S(2)}, u32[]{:S(2)}) collective-permute-start(bf16[4,640,128]{2,1,0:T(8,128)(2,1)S(1)} %get-tuple-element.147), channel_id=1, source_target_pairs={{0,8},{8,0},{16,24},{24,16},{1,9},{9,1},{17,25},{25,17},{2,10},{10... | collective-permute-start | bytes 1966088 | tf_op jit(solution)/shard_map/ppermute | solution.py:248
  6.8 7.3 %copy-start.3 = (s32[5120]{0:T(1024)S(1)}, s32[5120]{0:T(1024)}, u32[]{:S(2)}) copy-start(s32[5120]{0:T(1024)} %param.12) | copy-start | bytes 61444
  7.1 5.2 %collective-permute-start.10 = (s32[1,256]{1,0:T(1,128)S(1)}, s32[1,256]{1,0:T(1,128)S(1)}, u32[]{:S(2)}, u32[]{:S(2)}) collective-permute-start(s32[1,256]{1,0:T(1,128)S(1)} %shard_map.64.refs_0_.refs_1_), channel_id=1, source_target_pairs={{0,4},{1,5},{2,6},{3,7},{4,0},{5,1},{6,2},{7,3},{8,12},{9,13},{10,... | collective-permute-start | bytes 3080 | tf_op jit(solution)/shard_map/ppermute | solution.py:248
  12.3 3.6 %collective-permute-start.11 = (s32[2,256]{1,0:T(2,128)S(1)}, s32[2,256]{1,0:T(2,128)S(1)}, u32[]{:S(2)}, u32[]{:S(2)}) collective-permute-start(s32[2,256]{1,0:T(2,128)S(1)} %pad_add_fusion.1), channel_id=1, source_target_pairs={{0,1},{1,0},{2,3},{3,2},{4,5},{5,4},{6,7},{7,6},{8,9},{9,8},{10,11... | collective-permute-start | bytes 6152 | tf_op jit(solution)/shard_map/ppermute | solution.py:248
  16.4 14.8 %collective-permute-start.15 = (bf16[56,1024]{1,0:T(8,128)(2,1)S(1)}, bf16[56,1024]{1,0:T(8,128)(2,1)S(1)}, u32[]{:S(2)}, u32[]{:S(2)}) collective-permute-start(bf16[56,1024]{1,0:T(8,128)(2,1)S(1)} %get-tuple-element.150), channel_id=1, source_target_pairs={{0,5},{1,4},{2,7},{3,6},{4,1},{5,0},{6,3},{7,2},{8,13},{9,12},{10,... | collective-permute-start | bytes 344072 | tf_op jit(solution)/shard_map/ppermute | solution.py:248
  20.9 13.5 %collective-permute-start.14 = (bf16[56,1024]{1,0:T(8,128)(2,1)S(1)}, bf16[56,1024]{1,0:T(8,128)(2,1)S(1)}, u32[]{:S(2)}, u32[]{:S(2)}) collective-permute-start(bf16[56,1024]{1,0:T(8,128)(2,1)S(1)} %get-tuple-element.149), channel_id=1, source_target_pairs={{0,4},{1,5},{2,6},{3,7},{4,0},{5,1},{6,2},{7,3},{8,12},{9,13},{10,... | collective-permute-start | bytes 344072 | tf_op jit(solution)/shard_map/ppermute | solution.py:248
  21.3 3.6 %collective-permute-start.12 = (s32[4,256]{1,0:T(4,128)S(1)}, s32[4,256]{1,0:T(4,128)S(1)}, u32[]{:S(2)}, u32[]{:S(2)}) collective-permute-start(s32[4,256]{1,0:T(4,128)S(1)} %pad_add_fusion), channel_id=1, source_target_pairs={{0,2},{1,3},{2,0},{3,1},{4,6},{5,7},{6,4},{7,5},{8,10},{9,11},{10,... | collective-permute-start | bytes 12296 | tf_op jit(solution)/shard_map/ppermute | solution.py:248
  25.7 10.1 %collective-permute-start.16 = (bf16[56,1024]{1,0:T(8,128)(2,1)S(1)}, bf16[56,1024]{1,0:T(8,128)(2,1)S(1)}, u32[]{:S(2)}, u32[]{:S(2)}) collective-permute-start(bf16[56,1024]{1,0:T(8,128)(2,1)S(1)} %get-tuple-element.151), channel_id=1, source_target_pairs={{0,6},{1,7},{2,4},{3,5},{4,2},{5,3},{6,0},{7,1},{8,14},{9,15},{10,... | collective-permute-start | bytes 344072 | tf_op jit(solution)/shard_map/ppermute | solution.py:248
  29.7 6.8 %collective-permute-start.20 = (bf16[56,1024]{1,0:T(8,128)(2,1)S(1)}, bf16[56,1024]{1,0:T(8,128)(2,1)S(1)}, u32[]{:S(2)}, u32[]{:S(2)}) collective-permute-start(bf16[56,1024]{1,0:T(8,128)(2,1)S(1)} %get-tuple-element.156), channel_id=1, source_target_pairs={{0,1},{1,0},{2,3},{3,2},{4,5},{5,4},{6,7},{7,6},{8,9},{9,8},{10,11... | collective-permute-start | bytes 344072 | tf_op jit(solution)/shard_map/ppermute | solution.py:248
  30.2 8.2 %collective-permute-start.17 = (bf16[56,1024]{1,0:T(8,128)(2,1)S(1)}, bf16[56,1024]{1,0:T(8,128)(2,1)S(1)}, u32[]{:S(2)}, u32[]{:S(2)}) collective-permute-start(bf16[56,1024]{1,0:T(8,128)(2,1)S(1)} %get-tuple-element.153), channel_id=1, source_target_pairs={{0,7},{1,6},{2,5},{3,4},{4,3},{5,2},{6,1},{7,0},{8,15},{9,14},{10,... | collective-permute-start | bytes 344072 | tf_op jit(solution)/shard_map/ppermute | solution.py:248
  31.3 7.2 %collective-permute-start.18 = (bf16[56,1024]{1,0:T(8,128)(2,1)S(1)}, bf16[56,1024]{1,0:T(8,128)(2,1)S(1)}, u32[]{:S(2)}, u32[]{:S(2)}) collective-permute-start(bf16[56,1024]{1,0:T(8,128)(2,1)S(1)} %get-tuple-element.154), channel_id=1, source_target_pairs={{0,3},{1,2},{2,1},{3,0},{4,7},{5,6},{6,5},{7,4},{8,11},{9,10},{10,... | collective-permute-start | bytes 344072 | tf_op jit(solution)/shard_map/ppermute | solution.py:248
  34.4 5.3 %collective-permute-start.19 = (bf16[56,1024]{1,0:T(8,128)(2,1)S(1)}, bf16[56,1024]{1,0:T(8,128)(2,1)S(1)}, u32[]{:S(2)}, u32[]{:S(2)}) collective-permute-start(bf16[56,1024]{1,0:T(8,128)(2,1)S(1)} %get-tuple-element.155), channel_id=1, source_target_pairs={{0,2},{1,3},{2,0},{3,1},{4,6},{5,7},{6,4},{7,5},{8,10},{9,11},{10,... | collective-permute-start | bytes 344072 | tf_op jit(solution)/shard_map/ppermute | solution.py:248
  40.7 8.3 %copy-start.4 = (bf16[128]{0:T(256)(128)(2,1)S(1)}, bf16[128]{0:T(256)(128)(2,1)}, u32[]{:S(2)}) copy-start(bf16[128]{0:T(256)(128)(2,1)} %param.11) | copy-start | bytes 772
  40.7 4.7 %collective-permute-start.21 = (bf16[384,128]{1,0:T(8,128)(2,1)S(1)}, bf16[384,128]{1,0:T(8,128)(2,1)S(1)}, u32[]{:S(2)}, u32[]{:S(2)}) collective-permute-start(bf16[384,128]{1,0:T(8,128)(2,1)S(1)} %shard_map.71), channel_id=1, source_target_pairs={{0,16},{8,24},{16,0},{24,8},{1,17},{9,25},{17,1},{25,9},{2,18},{10... | collective-permute-start | bytes 294920 | tf_op jit(solution)/shard_map/ppermute | solution.py:248
  42.7 4.0 %collective-permute-start.22 = (bf16[128,128]{1,0:T(8,128)(2,1)S(1)}, bf16[128,128]{1,0:T(8,128)(2,1)S(1)}, u32[]{:S(2)}, u32[]{:S(2)}) collective-permute-start(bf16[128,128]{1,0:T(8,128)(2,1)S(1)} %shard_map.72), channel_id=1, source_target_pairs={{0,16},{8,24},{16,0},{24,8},{1,17},{9,25},{17,1},{25,9},{2,18},{10... | collective-permute-start | bytes 98312 | tf_op jit(solution)/shard_map/ppermute | solution.py:248
  45.4 2.6 %collective-permute-start.23 = (f32[384,128]{1,0:T(8,128)S(1)}, f32[384,128]{1,0:T(8,128)S(1)}, u32[]{:S(2)}, u32[]{:S(2)}) collective-permute-start(f32[384,128]{1,0:T(8,128)S(1)} %convert_add_fusion.refs_0_), channel_id=1, source_target_pairs={{0,8},{8,0},{16,24},{24,16},{1,9},{9,1},{17,25},{25,17},{2,10},{10... | collective-permute-start | bytes 589832 | tf_op jit(solution)/shard_map/ppermute | solution.py:248
  46.7 1.3 %collective-permute-start.24 = (f32[128,128]{1,0:T(8,128)S(1)}, f32[128,128]{1,0:T(8,128)S(1)}, u32[]{:S(2)}, u32[]{:S(2)}) collective-permute-start(f32[128,128]{1,0:T(8,128)S(1)} %convert_add_fusion.1.refs_1_), channel_id=1, source_target_pairs={{0,8},{8,0},{16,24},{24,16},{1,9},{9,1},{17,25},{25,17},{2,10},{10... | collective-permute-start | bytes 196616 | tf_op jit(solution)/shard_map/ppermute | solution.py:248

commit v2 on v1

--- a/solution.py
+++ b/solution.py
@@ -12,7 +12,9 @@
 NB = 128
 SMOOTH = 4
 LANES = 128
-MARK_FLOPS = 2 * 10**10
+FIRST_FLOPS = 2 * 10**10
+SENDS = [4, 1, 5, 2, 6, 3, 7]
+EARLY = [0, 4, 1, 5]
 ROUND_ROWS = 56
 
 F32, BF16, I32 = jnp.float32, jnp.bfloat16, jnp.int32
@@ -39,7 +41,13 @@
     return lax.broadcasted_iota(I32, shape, axis)
 
 
-def spectrum_kernel(core_ref, taps_ref, table_ref, raw_ref, keep_ref, give_ref, rows_ref, mat_ref, sem):
+def averaging_kernel(core_ref, out_ref):
+    shape = out_ref.shape
+    near = jnp.abs(iota(shape, 0) % NB - iota(shape, 1)) <= SMOOTH
+    out_ref[...] = jnp.where(near | (iota(shape, 1) >= NB), 1.0, 0.0).astype(BF16)
+
+
+def spectrum_kernel(core_ref, taps_ref, table_ref, sum_ref, raw_ref, keep_ref, give_ref, rows_ref, mat_ref, sem):
     windows = raw_ref.shape[0]
     copies = [pltpu.make_async_copy(raw_ref.at[w], rows_ref.at[w], sem.at[w]) for w in range(windows)]
     for copy in copies:
@@ -50,9 +58,7 @@
     toeplitz = pltpu.roll(jnp.broadcast_to(wide, (n, 2 * n)), 0, 1, stride=1, stride_axis=0).astype(BF16)
     for b in range(mat_ref.shape[0] // n):
         mat_ref[b * n : (b + 1) * n, :] = dot(toeplitz, table_ref[b * n : (b + 2) * n, :]).astype(BF16)
-    shape = (2 * NB, 2 * NB)
-    near = jnp.abs(iota(shape, 0) % NB - iota(shape, 1)) <= SMOOTH
-    averaging = jnp.where(near | (iota(shape, 1) >= NB), 1.0, 0.0).astype(BF16)
+    averaging = sum_ref[...]
     bins = iota((1, NB), 1)
     counts = jnp.minimum(bins, SMOOTH) + jnp.minimum(NB - 1 - bins, SMOOTH) + 1
     inverse = 1.0 / counts.astype(F32)
@@ -88,7 +94,12 @@
     return jnp.sum(value, axis=1, keepdims=True)
 
 
-def mark_kernel(high_count, pairs_ref, marks_ref):
+def mark_kernel(high_count, *refs):
+    for pairs_ref, marks_ref in zip(refs[: len(refs) // 2], refs[len(refs) // 2 :]):
+        mark(high_count, pairs_ref, marks_ref)
+
+
+def mark(high_count, pairs_ref, marks_ref):
     table = None
     for j in range(2):
         ids = pairs_ref[j : j + 1, :]
@@ -270,11 +281,13 @@
 def spectra(tm, core, raw_blocks, fir_taps):
     windows, rows, length = raw_blocks.shape
     table = jnp.asarray(table_of(length, fir_taps.shape[0]))
+    shape = jax.ShapeDtypeStruct((2 * NB, 2 * NB), BF16)
+    averaging = call(averaging_kernel, shape, flops=FIRST_FLOPS)(core)
     half = jax.ShapeDtypeStruct((windows, rows, NB), BF16)
     keep, give = pl.pallas_call(
         spectrum_kernel,
         out_shape=(half, half),
-        in_specs=[SMEM, VMEM, VMEM, pl.BlockSpec(memory_space=pl.ANY)],
+        in_specs=[SMEM, VMEM, VMEM, VMEM, pl.BlockSpec(memory_space=pl.ANY)],
         out_specs=(VMEM, VMEM),
         scratch_shapes=[
             pltpu.VMEM(raw_blocks.shape, BF16),
@@ -285,7 +298,7 @@
         cost_estimate=pl.CostEstimate(
             flops=2 * windows * rows * length * 2 * NB, bytes_accessed=2 * windows * rows * length, transcendentals=0
         ),
-    )(core, fir_taps.reshape(1, -1), table, raw_blocks)
+    )(core, fir_taps.reshape(1, -1), table, averaging, raw_blocks)
     return keep, swap(give, "tm", tm, 1)
 
 
@@ -356,8 +369,11 @@
 
 def arrivals(n):
     _, known, _ = steps_of(n)
-    sends = [k for ks in known for k in sorted(ks) if k >= n // 2] + list(range(n // 2 - 1, 0, -1))
-    return sends, [0] + sends[: n // 2 - 1], sends[n // 2 - 1 :]
+    far = [k for ks in known for k in sorted(ks) if k >= n // 2]
+    near = list(range(n // 2 - 1, 0, -1))
+    sends = SENDS if n == 8 else far[:-1] + near + far[-1:]
+    early = EARLY if n == 8 else [0] + sends[: n // 2 - 1]
+    return sends, early, [k for k in sends if k not in early]
 
 
 def local(tm, n, raw_blocks, fir_taps, recorder_channel, pairs):
@@ -375,13 +391,15 @@
     _, early, late = arrivals(n)
 
     mark_shape = shaped((1, -(-high_count // 32) * LANES), I32)
-    own = call(functools.partial(mark_kernel, high_count), mark_shape, flops=MARK_FLOPS, smem=0)(pairs.T)
     keep, other = spectra(tm, core, raw_blocks, fir_taps)
+    theirs = swap(pairs.T, "chan", n, bits[0])
+    own, new = call(functools.partial(mark_kernel, high_count), [mark_shape] * 2, smem=0)(pairs.T, theirs)
 
     marks = [own]
     arrived = [None] * n
     for i, bit in enumerate(bits):
-        new = swap(jnp.concatenate(marks), "chan", n, bit)
+        if i:
+            new = swap(jnp.concatenate(marks), "chan", n, bit)
         here = [new] if i else [new, own]
         marks.append(new)
         owners = known[i] if i else known[i] + [0]
@@ -402,7 +420,7 @@
         smem=0,
     )(pick_early, *[arrived[k] for k in early])
 
-    sizes = [pair_count * 3 // 4, pair_count // 4]
+    sizes = [pair_count * 5 // 8, pair_count * 3 // 8]
     totals, seconds = [], []
     for i, size in enumerate(sizes):
         total = call(

time: 49.2 us -> 50 us (1.016)
  Pallas kernels: 11.7 us -> 9.96 us
  starting transfers between devices: 20.4 us -> 22.1 us
  local copies, waits for them, and re-layouts: 1.08 us -> 2.65 us
  waiting for transfers between devices: 15 us -> 14.3 us
    pallas_call x1, Pallas kernels: 5.2 us -> 3.34 us  [spectra(): pl.pallas_call(spectrum_kernel, out_shape=(half, half), in_specs=[SMEM, V...]
    ppermute x15, starting transfers between devices: 20.4 us -> 22.1 us  [swap(): return lax.ppermute(value, axis, [(i, i ^ bit) for i in range(size)])]
    unnamed x8 -> x10, local copies, waits for them, and re-layouts: 1.08 us -> 2.64 us
    ppermute x15, waiting for transfers between devices: 15 us -> 14.3 us  [swap(): return lax.ppermute(value, axis, [(i, i ^ bit) for i in range(size)])]
    pallas_call x9 -> x10, Pallas kernels: 6.55 us -> 6.63 us  [run(): pl.pallas_call(kernel, out_shape=tuple(out) if many else out, in_specs=sp...]
  transfers between devices with their start and end apart: 15 -> 15, of which waited for: 10 -> 9; matrix products, arithmetic and copies ran while one was open for 0% -> 0% of each run, Pallas kernels for 8% -> 8%
where the time goes in v2:
time: 50 us; the launch traced here: 49.8 us
  starting transfers between devices  22.1 us (44%)
  waiting for transfers between devices  14.3 us (29%)
  Pallas kernels  9.96 us (20%)
  local copies, waits for them, and re-layouts  2.65 us (5%)
  between operations  0.81 us (2%)
    ppermute x15, starting transfers between devices, swap(): return lax.ppermute(value, axis, [(i, i ^ bit) for i in range(size)])  22.1 us
    ppermute x15, waiting for transfers between devices, swap(): return lax.ppermute(value, axis, [(i, i ^ bit) for i in range(size)])  14.3 us
    pallas_call x10, Pallas kernels, run(): pl.pallas_call(kernel, out_shape=tuple(out) if many else out, in_specs=sp...  6.63 us
    pallas_call x1, Pallas kernels, spectra(): pl.pallas_call(spectrum_kernel, out_shape=(half, half), in_specs=[SMEM, V...  3.34 us
    unnamed x10, local copies, waits for them, and re-layouts  2.64 us
  transfers between devices with their start and end apart: 15, of which 9 were waited for; matrix products, arithmetic and copies ran while one was open for 0% of the time, Pallas kernels for 8%

profile of v2, /device:TPU:0, one launch (start us, length us, event | category | flops | bytes accessed | tf_op | source)
XLA Modules:
  0.0 49.8 jit_solution(9526428271980489101)
XLA Ops:
  0.1 1.0 %copy-done.1 = bf16[1152,256]{1,0:T(8,128)(2,1)S(1)} copy-done((bf16[1152,256]{1,0:T(8,128)(2,1)S(1)}, bf16[1152,256]{1,0:T(8,128)(2,1)}, u32[]{:S(2)}) %copy-start.1) | copy-done | bytes 589848
  1.1 1.6 %copy-done.2 = bf16[4,640,1024]{2,1,0:T(8,128)(2,1)S(1)} copy-done((bf16[4,640,1024]{2,1,0:T(8,128)(2,1)S(1)}, bf16[4,640,1024]{2,1,0:T(8,128)(2,1)}, u32[]{:S(2)}) %copy-start.2) | copy-done | bytes 5242904
  2.7 3.3 %shard_map.67 = (bf16[4,640,128]{2,1,0:T(8,128)(2,1)S(1)}, bf16[4,640,128]{2,1,0:T(8,128)(2,1)S(1)}) custom-call(s32[1]{0:T(128)} %bitcast.3.core_ref, bf16[1,128]{1,0:T(2,128)(2,1)S(1)} %bitcast.105, bf16[1152,256]{1,0:T(8,128)(2,1)S(1)} %copy-done.1, bf16[256,256]{1,0:T(8,128)(2,1)S(1)} %shard_map.66.sum_ref, bf16[4,640,1024]{2,1,0:T(8,128)(2,1)S(1)} %copy-done.2), custom_call_target="tpu_custom_call" | custom-call | flops 1342177280 | bytes 5242880 | tf_op jit(solution)/shard_map/pallas_call | solution.py:287
  6.6 3.7 %collective-permute-start.10 = (s32[2,512]{1,0:T(2,128)S(1)}, s32[2,512]{1,0:T(2,128)S(1)}, u32[]{:S(2)}, u32[]{:S(2)}) collective-permute-start(s32[2,512]{1,0:T(2,128)S(1)} %bitcast.100), channel_id=1, source_target_pairs={{0,4},{1,5},{2,6},{3,7},{4,0},{5,1},{6,2},{7,3},{8,12},{9,13},{10,... | collective-permute-start | bytes 12296 | tf_op jit(solution)/shard_map/ppermute | solution.py:259
  10.3 1.6 %collective-permute-done.10.refs_1_ = s32[2,512]{1,0:T(2,128)S(1)} collective-permute-done((s32[2,512]{1,0:T(2,128)S(1)}, s32[2,512]{1,0:T(2,128)S(1)}, u32[]{:S(2)}, u32[]{:S(2)}) %collective-permute-start.10) | collective-permute-done | bytes 4128 | tf_op jit(solution)/shard_map/ppermute | solution.py:259
  12.2 1.9 %collective-permute-start.11 = (s32[2,256]{1,0:T(2,128)S(1)}, s32[2,256]{1,0:T(2,128)S(1)}, u32[]{:S(2)}, u32[]{:S(2)}) collective-permute-start(s32[2,256]{1,0:T(2,128)S(1)} %pad_add_fusion.1), channel_id=1, source_target_pairs={{0,1},{1,0},{2,3},{3,2},{4,5},{5,4},{6,7},{7,6},{8,9},{9,8},{10,11... | collective-permute-start | bytes 6152 | tf_op jit(solution)/shard_map/ppermute | solution.py:259
  14.1 1.7 %collective-permute-done.11.refs_2_.refs_0_ = s32[2,256]{1,0:T(2,128)S(1)} collective-permute-done((s32[2,256]{1,0:T(2,128)S(1)}, s32[2,256]{1,0:T(2,128)S(1)}, u32[]{:S(2)}, u32[]{:S(2)}) %collective-permute-start.11) | collective-permute-done | bytes 2080 | tf_op jit(solution)/shard_map/ppermute | solution.py:259
  16.4 1.9 %collective-permute-start.15 = (bf16[56,1024]{1,0:T(8,128)(2,1)S(1)}, bf16[56,1024]{1,0:T(8,128)(2,1)S(1)}, u32[]{:S(2)}, u32[]{:S(2)}) collective-permute-start(bf16[56,1024]{1,0:T(8,128)(2,1)S(1)} %get-tuple-element.154), channel_id=1, source_target_pairs={{0,1},{1,0},{2,3},{3,2},{4,5},{5,4},{6,7},{7,6},{8,9},{9,8},{10,11... | collective-permute-start | bytes 344072 | tf_op jit(solution)/shard_map/ppermute | solution.py:259
  18.3 2.5 %collective-permute-start.16 = (bf16[56,1024]{1,0:T(8,128)(2,1)S(1)}, bf16[56,1024]{1,0:T(8,128)(2,1)S(1)}, u32[]{:S(2)}, u32[]{:S(2)}) collective-permute-start(bf16[56,1024]{1,0:T(8,128)(2,1)S(1)} %get-tuple-element.155), channel_id=1, source_target_pairs={{0,5},{1,4},{2,7},{3,6},{4,1},{5,0},{6,3},{7,2},{8,13},{9,12},{10,... | collective-permute-start | bytes 344072 | tf_op jit(solution)/shard_map/ppermute | solution.py:259
  21.5 1.9 %collective-permute-start.12 = (s32[4,256]{1,0:T(4,128)S(1)}, s32[4,256]{1,0:T(4,128)S(1)}, u32[]{:S(2)}, u32[]{:S(2)}) collective-permute-start(s32[4,256]{1,0:T(4,128)S(1)} %pad_add_fusion), channel_id=1, source_target_pairs={{0,2},{1,3},{2,0},{3,1},{4,6},{5,7},{6,4},{7,5},{8,10},{9,11},{10,... | collective-permute-start | bytes 12296 | tf_op jit(solution)/shard_map/ppermute | solution.py:259
  23.3 1.8 %collective-permute-done.12.refs_3_.refs_0_ = s32[4,256]{1,0:T(4,128)S(1)} collective-permute-done((s32[4,256]{1,0:T(4,128)S(1)}, s32[4,256]{1,0:T(4,128)S(1)}, u32[]{:S(2)}, u32[]{:S(2)}) %collective-permute-start.12) | collective-permute-done | bytes 4128 | tf_op jit(solution)/shard_map/ppermute | solution.py:259
  25.9 1.9 %collective-permute-start.17 = (bf16[56,1024]{1,0:T(8,128)(2,1)S(1)}, bf16[56,1024]{1,0:T(8,128)(2,1)S(1)}, u32[]{:S(2)}, u32[]{:S(2)}) collective-permute-start(bf16[56,1024]{1,0:T(8,128)(2,1)S(1)} %get-tuple-element.157), channel_id=1, source_target_pairs={{0,2},{1,3},{2,0},{3,1},{4,6},{5,7},{6,4},{7,5},{8,10},{9,11},{10,... | collective-permute-start | bytes 344072 | tf_op jit(solution)/shard_map/ppermute | solution.py:259
  27.7 3.3 %collective-permute-start.18 = (bf16[56,1024]{1,0:T(8,128)(2,1)S(1)}, bf16[56,1024]{1,0:T(8,128)(2,1)S(1)}, u32[]{:S(2)}, u32[]{:S(2)}) collective-permute-start(bf16[56,1024]{1,0:T(8,128)(2,1)S(1)} %get-tuple-element.158), channel_id=1, source_target_pairs={{0,6},{1,7},{2,4},{3,5},{4,2},{5,3},{6,0},{7,1},{8,14},{9,15},{10,... | collective-permute-start | bytes 344072 | tf_op jit(solution)/shard_map/ppermute | solution.py:259
  31.0 1.2 %collective-permute-start.19 = (bf16[56,1024]{1,0:T(8,128)(2,1)S(1)}, bf16[56,1024]{1,0:T(8,128)(2,1)S(1)}, u32[]{:S(2)}, u32[]{:S(2)}) collective-permute-start(bf16[56,1024]{1,0:T(8,128)(2,1)S(1)} %get-tuple-element.159), channel_id=1, source_target_pairs={{0,3},{1,2},{2,1},{3,0},{4,7},{5,6},{6,5},{7,4},{8,11},{9,10},{10,... | collective-permute-start | bytes 344072 | tf_op jit(solution)/shard_map/ppermute | solution.py:259
  32.3 0.9 %collective-permute-start.20 = (bf16[56,1024]{1,0:T(8,128)(2,1)S(1)}, bf16[56,1024]{1,0:T(8,128)(2,1)S(1)}, u32[]{:S(2)}, u32[]{:S(2)}) collective-permute-start(bf16[56,1024]{1,0:T(8,128)(2,1)S(1)} %get-tuple-element.160), channel_id=1, source_target_pairs={{0,7},{1,6},{2,5},{3,4},{4,3},{5,2},{6,1},{7,0},{8,15},{9,14},{10,... | collective-permute-start | bytes 344072 | tf_op jit(solution)/shard_map/ppermute | solution.py:259
  33.1 1.4 %shard_map.65 = (bf16[1024,224]{1,0:T(8,128)(2,1)S(1)}, bf16[1024,224]{1,0:T(8,128)(2,1)S(1)}, s32[1,1]{1,0:T(1,128)}) custom-call(s32[1]{0:T(128)} %bitcast.me_ref, s32[1,256]{1,0:T(1,128)S(1)} %get-tuple-element.464.refs_0_.refs_1_, s32[1,256]{1,0:T(1,128)S(1)} %get-tuple-element.465.refs_1_.refs_0_, s32[2,256]{1,0:T(2,128)S(1)} %collective-permute-done.11.refs_2_.refs_0_, ...), custom_call_target="tpu_custom_call" | custom-call | bytes 950280 | tf_op jit(solution)/shard_map/pallas_call | solution.py:268
  35.2 1.7 %collective-permute-done.18.refs_1_ = bf16[56,1024]{1,0:T(8,128)(2,1)S(1)} collective-permute-done((bf16[56,1024]{1,0:T(8,128)(2,1)S(1)}, bf16[56,1024]{1,0:T(8,128)(2,1)S(1)}, u32[]{:S(2)}, u32[]{:S(2)}) %collective-permute-start.18) | collective-permute-done | bytes 114720 | tf_op jit(solution)/shard_map/ppermute | solution.py:259
  37.0 1.8 %collective-permute-done.19.refs_2_ = bf16[56,1024]{1,0:T(8,128)(2,1)S(1)} collective-permute-done((bf16[56,1024]{1,0:T(8,128)(2,1)S(1)}, bf16[56,1024]{1,0:T(8,128)(2,1)S(1)}, u32[]{:S(2)}, u32[]{:S(2)}) %collective-permute-start.19) | collective-permute-done | bytes 114720 | tf_op jit(solution)/shard_map/ppermute | solution.py:259
  38.8 1.5 %collective-permute-done.20.refs_3_ = bf16[56,1024]{1,0:T(8,128)(2,1)S(1)} collective-permute-done((bf16[56,1024]{1,0:T(8,128)(2,1)S(1)}, bf16[56,1024]{1,0:T(8,128)(2,1)S(1)}, u32[]{:S(2)}, u32[]{:S(2)}) %collective-permute-start.20) | collective-permute-done | bytes 114720 | tf_op jit(solution)/shard_map/ppermute | solution.py:259
  40.3 0.8 %shard_map.72 = bf16[320,128]{1,0:T(8,128)(2,1)S(1)} custom-call(bf16[1024,1024]{1,0:T(8,128)(2,1)S(1)} %shard_map.70.early_ref, bf16[1024,224]{1,0:T(8,128)(2,1)S(1)} %get-tuple-element.156.gather_ref, bf16[56,1024]{1,0:T(8,128)(2,1)S(1)} %collective-permute-done.17.refs_0_, bf16[56,1024]{1,0:T(8,128)(2,1)S(1)} %collective-permute-done.18.refs_1_, ...), custom_call_target="tpu_custom_call" | custom-call | flops 293601280 | bytes 3096576 | tf_op jit(solution)/shard_map/pallas_call | solution.py:268
  41.1 1.5 %collective-permute-start.21 = (bf16[320,128]{1,0:T(8,128)(2,1)S(1)}, bf16[320,128]{1,0:T(8,128)(2,1)S(1)}, u32[]{:S(2)}, u32[]{:S(2)}) collective-permute-start(bf16[320,128]{1,0:T(8,128)(2,1)S(1)} %shard_map.72), channel_id=1, source_target_pairs={{0,16},{8,24},{16,0},{24,8},{1,17},{9,25},{17,1},{25,9},{2,18},{10... | collective-permute-start | bytes 245768 | tf_op jit(solution)/shard_map/ppermute | solution.py:259
  43.9 1.8 %collective-permute-done.21 = bf16[320,128]{1,0:T(8,128)(2,1)S(1)} collective-permute-done((bf16[320,128]{1,0:T(8,128)(2,1)S(1)}, bf16[320,128]{1,0:T(8,128)(2,1)S(1)}, u32[]{:S(2)}, u32[]{:S(2)}) %collective-permute-start.21) | collective-permute-done | bytes 81952 | tf_op jit(solution)/shard_map/ppermute | solution.py:259
  45.8 1.7 %collective-permute-done.22 = bf16[192,128]{1,0:T(8,128)(2,1)S(1)} collective-permute-done((bf16[192,128]{1,0:T(8,128)(2,1)S(1)}, bf16[192,128]{1,0:T(8,128)(2,1)S(1)}, u32[]{:S(2)}, u32[]{:S(2)}) %collective-permute-start.22) | collective-permute-done | bytes 49184 | tf_op jit(solution)/shard_map/ppermute | solution.py:259
  48.8 1.0 %shard_map.74 = f32[512,256]{1,0:T(8,128)} custom-call(s32[1]{0:T(128)} %bitcast.3.core_ref, f32[320,128]{1,0:T(8,128)S(1)} %convert_add_fusion.refs_0_, f32[192,128]{1,0:T(8,128)S(1)} %convert_add_fusion.1.refs_1_, f32[320,128]{1,0:T(8,128)S(1)} %collective-permute-done.23.refs_2_, f32[192,128]{1,0:T(8,128)S(1)} %collective-permute-done.24.refs_3_), custom_call_target="tpu_custom_call" | custom-call | bytes 1048580 | tf_op jit(solution)/shard_map/pallas_call | solution.py:268
  (33 shorter events, 5.5 us)
Async XLA Ops:
  0.0 1.1 %copy-start.1 = (bf16[1152,256]{1,0:T(8,128)(2,1)S(1)}, bf16[1152,256]{1,0:T(8,128)(2,1)}, u32[]{:S(2)}) copy-start(bf16[1152,256]{1,0:T(8,128)(2,1)} %constant.231.clone.table_ref) | copy-start | bytes 1769476
  0.0 2.7 %copy-start.2 = (bf16[4,640,1024]{2,1,0:T(8,128)(2,1)S(1)}, bf16[4,640,1024]{2,1,0:T(8,128)(2,1)}, u32[]{:S(2)}) copy-start(bf16[4,640,1024]{2,1,0:T(8,128)(2,1)} %raw_ref.1) | copy-start | bytes 15728644
  0.0 2.7 %copy-start.7 = (bf16[128]{0:T(256)(128)(2,1)S(1)}, bf16[128]{0:T(256)(128)(2,1)}, u32[]{:S(2)}) copy-start(bf16[128]{0:T(256)(128)(2,1)} %param.11) | copy-start | bytes 772
  2.7 3.9 %copy-start.4 = (s32[512,2]{0,1:T(2,128)S(1)}, s32[512,2]{0,1:T(2,128)}, u32[]{:S(2)}) copy-start(s32[512,2]{0,1:T(2,128)} %param.13) | copy-start | bytes 12292
  2.7 11.4 %copy-start.6 = (s32[5120]{0:T(1024)S(1)}, s32[5120]{0:T(1024)}, u32[]{:S(2)}) copy-start(s32[5120]{0:T(1024)} %param.12) | copy-start | bytes 61444
  6.0 9.8 %collective-permute-start.13 = (bf16[4,640,128]{2,1,0:T(8,128)(2,1)S(1)}, bf16[4,640,128]{2,1,0:T(8,128)(2,1)S(1)}, u32[]{:S(2)}, u32[]{:S(2)}) collective-permute-start(bf16[4,640,128]{2,1,0:T(8,128)(2,1)S(1)} %get-tuple-element.151), channel_id=1, source_target_pairs={{0,8},{8,0},{16,24},{24,16},{1,9},{9,1},{17,25},{25,17},{2,10},{10... | collective-permute-start | bytes 1966088 | tf_op jit(solution)/shard_map/ppermute | solution.py:259
  6.6 5.2 %collective-permute-start.10 = (s32[2,512]{1,0:T(2,128)S(1)}, s32[2,512]{1,0:T(2,128)S(1)}, u32[]{:S(2)}, u32[]{:S(2)}) collective-permute-start(s32[2,512]{1,0:T(2,128)S(1)} %bitcast.100), channel_id=1, source_target_pairs={{0,4},{1,5},{2,6},{3,7},{4,0},{5,1},{6,2},{7,3},{8,12},{9,13},{10,... | collective-permute-start | bytes 12296 | tf_op jit(solution)/shard_map/ppermute | solution.py:259
  12.2 3.7 %collective-permute-start.11 = (s32[2,256]{1,0:T(2,128)S(1)}, s32[2,256]{1,0:T(2,128)S(1)}, u32[]{:S(2)}, u32[]{:S(2)}) collective-permute-start(s32[2,256]{1,0:T(2,128)S(1)} %pad_add_fusion.1), channel_id=1, source_target_pairs={{0,1},{1,0},{2,3},{3,2},{4,5},{5,4},{6,7},{7,6},{8,9},{9,8},{10,11... | collective-permute-start | bytes 6152 | tf_op jit(solution)/shard_map/ppermute | solution.py:259
  16.4 14.7 %collective-permute-start.15 = (bf16[56,1024]{1,0:T(8,128)(2,1)S(1)}, bf16[56,1024]{1,0:T(8,128)(2,1)S(1)}, u32[]{:S(2)}, u32[]{:S(2)}) collective-permute-start(bf16[56,1024]{1,0:T(8,128)(2,1)S(1)} %get-tuple-element.154), channel_id=1, source_target_pairs={{0,1},{1,0},{2,3},{3,2},{4,5},{5,4},{6,7},{7,6},{8,9},{9,8},{10,11... | collective-permute-start | bytes 344072 | tf_op jit(solution)/shard_map/ppermute | solution.py:259
  18.3 14.0 %collective-permute-start.16 = (bf16[56,1024]{1,0:T(8,128)(2,1)S(1)}, bf16[56,1024]{1,0:T(8,128)(2,1)S(1)}, u32[]{:S(2)}, u32[]{:S(2)}) collective-permute-start(bf16[56,1024]{1,0:T(8,128)(2,1)S(1)} %get-tuple-element.155), channel_id=1, source_target_pairs={{0,5},{1,4},{2,7},{3,6},{4,1},{5,0},{6,3},{7,2},{8,13},{9,12},{10,... | collective-permute-start | bytes 344072 | tf_op jit(solution)/shard_map/ppermute | solution.py:259
  21.4 13.1 %collective-permute-start.14 = (bf16[56,1024]{1,0:T(8,128)(2,1)S(1)}, bf16[56,1024]{1,0:T(8,128)(2,1)S(1)}, u32[]{:S(2)}, u32[]{:S(2)}) collective-permute-start(bf16[56,1024]{1,0:T(8,128)(2,1)S(1)} %get-tuple-element.153), channel_id=1, source_target_pairs={{0,4},{1,5},{2,6},{3,7},{4,0},{5,1},{6,2},{7,3},{8,12},{9,13},{10,... | collective-permute-start | bytes 344072 | tf_op jit(solution)/shard_map/ppermute | solution.py:259
  21.5 3.7 %collective-permute-start.12 = (s32[4,256]{1,0:T(4,128)S(1)}, s32[4,256]{1,0:T(4,128)S(1)}, u32[]{:S(2)}, u32[]{:S(2)}) collective-permute-start(s32[4,256]{1,0:T(4,128)S(1)} %pad_add_fusion), channel_id=1, source_target_pairs={{0,2},{1,3},{2,0},{3,1},{4,6},{5,7},{6,4},{7,5},{8,10},{9,11},{10,... | collective-permute-start | bytes 12296 | tf_op jit(solution)/shard_map/ppermute | solution.py:259
  25.9 9.4 %collective-permute-start.17 = (bf16[56,1024]{1,0:T(8,128)(2,1)S(1)}, bf16[56,1024]{1,0:T(8,128)(2,1)S(1)}, u32[]{:S(2)}, u32[]{:S(2)}) collective-permute-start(bf16[56,1024]{1,0:T(8,128)(2,1)S(1)} %get-tuple-element.157), channel_id=1, source_target_pairs={{0,2},{1,3},{2,0},{3,1},{4,6},{5,7},{6,4},{7,5},{8,10},{9,11},{10,... | collective-permute-start | bytes 344072 | tf_op jit(solution)/shard_map/ppermute | solution.py:259
  27.7 9.3 %collective-permute-start.18 = (bf16[56,1024]{1,0:T(8,128)(2,1)S(1)}, bf16[56,1024]{1,0:T(8,128)(2,1)S(1)}, u32[]{:S(2)}, u32[]{:S(2)}) collective-permute-start(bf16[56,1024]{1,0:T(8,128)(2,1)S(1)} %get-tuple-element.158), channel_id=1, source_target_pairs={{0,6},{1,7},{2,4},{3,5},{4,2},{5,3},{6,0},{7,1},{8,14},{9,15},{10,... | collective-permute-start | bytes 344072 | tf_op jit(solution)/shard_map/ppermute | solution.py:259
  31.0 7.8 %collective-permute-start.19 = (bf16[56,1024]{1,0:T(8,128)(2,1)S(1)}, bf16[56,1024]{1,0:T(8,128)(2,1)S(1)}, u32[]{:S(2)}, u32[]{:S(2)}) collective-permute-start(bf16[56,1024]{1,0:T(8,128)(2,1)S(1)} %get-tuple-element.159), channel_id=1, source_target_pairs={{0,3},{1,2},{2,1},{3,0},{4,7},{5,6},{6,5},{7,4},{8,11},{9,10},{10,... | collective-permute-start | bytes 344072 | tf_op jit(solution)/shard_map/ppermute | solution.py:259
  32.3 8.1 %collective-permute-start.20 = (bf16[56,1024]{1,0:T(8,128)(2,1)S(1)}, bf16[56,1024]{1,0:T(8,128)(2,1)S(1)}, u32[]{:S(2)}, u32[]{:S(2)}) collective-permute-start(bf16[56,1024]{1,0:T(8,128)(2,1)S(1)} %get-tuple-element.160), channel_id=1, source_target_pairs={{0,7},{1,6},{2,5},{3,4},{4,3},{5,2},{6,1},{7,0},{8,15},{9,14},{10,... | collective-permute-start | bytes 344072 | tf_op jit(solution)/shard_map/ppermute | solution.py:259
  41.1 4.5 %collective-permute-start.21 = (bf16[320,128]{1,0:T(8,128)(2,1)S(1)}, bf16[320,128]{1,0:T(8,128)(2,1)S(1)}, u32[]{:S(2)}, u32[]{:S(2)}) collective-permute-start(bf16[320,128]{1,0:T(8,128)(2,1)S(1)} %shard_map.72), channel_id=1, source_target_pairs={{0,16},{8,24},{16,0},{24,8},{1,17},{9,25},{17,1},{25,9},{2,18},{10... | collective-permute-start | bytes 245768 | tf_op jit(solution)/shard_map/ppermute | solution.py:259
  43.3 4.2 %collective-permute-start.22 = (bf16[192,128]{1,0:T(8,128)(2,1)S(1)}, bf16[192,128]{1,0:T(8,128)(2,1)S(1)}, u32[]{:S(2)}, u32[]{:S(2)}) collective-permute-start(bf16[192,128]{1,0:T(8,128)(2,1)S(1)} %shard_map.73), channel_id=1, source_target_pairs={{0,16},{8,24},{16,0},{24,8},{1,17},{9,25},{17,1},{25,9},{2,18},{10... | collective-permute-start | bytes 147464 | tf_op jit(solution)/shard_map/ppermute | solution.py:259
  45.7 3.1 %collective-permute-start.23 = (f32[320,128]{1,0:T(8,128)S(1)}, f32[320,128]{1,0:T(8,128)S(1)}, u32[]{:S(2)}, u32[]{:S(2)}) collective-permute-start(f32[320,128]{1,0:T(8,128)S(1)} %convert_add_fusion.refs_0_), channel_id=1, source_target_pairs={{0,8},{8,0},{16,24},{24,16},{1,9},{9,1},{17,25},{25,17},{2,10},{10... | collective-permute-start | bytes 491528 | tf_op jit(solution)/shard_map/ppermute | solution.py:259
  47.4 1.4 %collective-permute-start.24 = (f32[192,128]{1,0:T(8,128)S(1)}, f32[192,128]{1,0:T(8,128)S(1)}, u32[]{:S(2)}, u32[]{:S(2)}) collective-permute-start(f32[192,128]{1,0:T(8,128)S(1)} %convert_add_fusion.1.refs_1_), channel_id=1, source_target_pairs={{0,8},{8,0},{16,24},{24,16},{1,9},{9,1},{17,25},{25,17},{2,10},{10... | collective-permute-start | bytes 294920 | tf_op jit(solution)/shard_map/ppermute | solution.py:259

commit v3 on v2

--- a/solution.py
+++ b/solution.py
@@ -13,9 +13,9 @@
 SMOOTH = 4
 LANES = 128
 FIRST_FLOPS = 2 * 10**10
-SENDS = [4, 1, 5, 2, 6, 3, 7]
+SENDS = [4, 1, 5, 2, 3, 6, 7]
 EARLY = [0, 4, 1, 5]
-ROUND_ROWS = 56
+ROUND_ROWS = 52
 
 F32, BF16, I32 = jnp.float32, jnp.bfloat16, jnp.int32
 VMEM = pl.BlockSpec(memory_space=pltpu.VMEM)
@@ -142,6 +142,26 @@
     return jnp.concatenate(out, axis=1), count
 
 
+def padded(chunk):
+    return -(-chunk // 8) * 8
+
+
+def folded(chunk, width):
+    fold = 1
+    while chunk * fold % 8:
+        fold *= 2
+    return chunk * fold, width // fold
+
+
+def lay_out(chunk, chunk_refs, rows_ref):
+    stride, part = padded(chunk), chunk_refs[0].shape[1]
+    for k, ref in enumerate(chunk_refs):
+        for p in range(rows_ref.shape[1] // part):
+            rows_ref[k * stride : k * stride + chunk, p * part : (p + 1) * part] = ref[p * chunk : (p + 1) * chunk, :]
+        if stride > chunk:
+            rows_ref[k * stride + chunk : (k + 1) * stride, :] = jnp.zeros((stride - chunk, rows_ref.shape[1]), BF16)
+
+
 def spread(row, count):
     return jnp.broadcast_to(row, (count, row.shape[1]))
 
@@ -154,22 +174,30 @@
     return marks
 
 
-def pack_kernel(lines, pieces, me_ref, *refs):
+def pack_kernel(lines, pieces, chunk, me_ref, *refs):
     marks = stacked(refs[:pieces])
     chan_ref, keep_ref, other_ref = refs[pieces : pieces + 3]
     chunk_refs = refs[pieces + 3 :]
-    chunk = chunk_refs[0].shape[0]
+    part, stride = chunk_refs[0].shape[1], padded(chunk)
     rows = chan_ref.shape[1]
     ids = spread(chan_ref[pl.ds(me_ref[0], 1), :], marks.shape[0])
     place, _ = places(wanted(marks, ids))
-    slots = iota((chunk, rows), 0)
+    slots = iota((stride, rows), 0)
     select = [(slots == place[i : i + 1, :]).astype(F32).astype(BF16) for i in lines]
     select = jnp.concatenate(select, axis=0)
     for w in range(keep_ref.shape[0]):
         data = jnp.concatenate([keep_ref[w], other_ref[w]], axis=1)
         out = dot(select, data).astype(BF16)
+        fold, lane = 2 * w * LANES // part * chunk, 2 * w * LANES % part
         for i in range(len(lines)):
-            chunk_refs[i][:, 2 * w * LANES : 2 * (w + 1) * LANES] = out[i * chunk : (i + 1) * chunk]
+            chunk_refs[i][fold : fold + chunk, lane : lane + 2 * LANES] = out[i * stride : i * stride + chunk]
+
+
+def tables_kernel(n, me_ref, *refs):
+    marks = stacked(refs[:-3])[:n]
+    chan_ref, place_ref, rank_ref = refs[-3:]
+    place_ref[...], _ = places(wanted(marks, spread(chan_ref[pl.ds(me_ref[0], 1), :], n)))
+    rank_ref[...], _ = places(wanted(spread(marks[:1], n), chan_ref[...]))
 
 
 def arrival_kernel(sources, chunk, pieces, me_ref, *refs):
@@ -186,17 +214,19 @@
             count = lane_sum(sum(parts).astype(F32))
         most = count if most is None else jnp.maximum(most, count)
     most_ref[...] = jnp.max(most, axis=0, keepdims=True).astype(I32)
-    slots = iota((chunk, ids.shape[1]), 0)
+    stride = padded(chunk)
+    slots = iota((stride, ids.shape[1]), 0)
+    slots = jnp.where(slots < chunk, slots, -2)
     here = []
     for s in range(n):
         held = jnp.where(slots == place[s : s + 1, :], ids[s : s + 1, :] + 1, 0)
         here.append(lane_sum(held.astype(F32)))
     column = jnp.concatenate(here, axis=0) - 1.0
-    row = jnp.broadcast_to(column, (n * chunk, LANES)).T[:1, :]
+    row = jnp.broadcast_to(column, (n * stride, LANES)).T[:1, :]
     ends = pairs_ref[...].astype(F32)
     count = ends.shape[1]
     ends = jnp.concatenate([ends, jnp.zeros((6, count), F32)], axis=0).T
-    middle = n // 2 * chunk
+    middle = n // 2 * stride
     for j in range(2):
         match = ends[:, j : j + 1] == row
         match = jnp.where(match, 1.0, 0.0).astype(BF16)
@@ -204,20 +234,16 @@
         late_ref[j * count : (j + 1) * count, :] = match[:, middle:]
 
 
-def early_kernel(half, gather_ref, *refs):
+def early_kernel(half, chunk, gather_ref, *refs):
     chunk_refs, out_ref, rows_ref = refs[:half], refs[half], refs[half + 1]
-    chunk = chunk_refs[0].shape[0]
-    for k in range(half):
-        rows_ref[k * chunk : (k + 1) * chunk, :] = chunk_refs[k][...]
+    lay_out(chunk, chunk_refs, rows_ref)
     for w in range(0, rows_ref.shape[1], 2 * LANES):
         out_ref[:, w : w + 2 * LANES] = dot(gather_ref[...], rows_ref[:, w : w + 2 * LANES]).astype(BF16)
 
 
-def product_kernel(half, start, early_ref, gather_ref, *refs):
+def product_kernel(half, chunk, start, early_ref, gather_ref, *refs):
     chunk_refs, out_ref, rows_ref = refs[:half], refs[half], refs[half + 1]
-    chunk = chunk_refs[0].shape[0]
-    for k in range(half):
-        rows_ref[k * chunk : (k + 1) * chunk, :] = chunk_refs[k][...]
+    lay_out(chunk, chunk_refs, rows_ref)
     count = out_ref.shape[0]
     total = gather_ref.shape[0] // 2
     pick = jnp.concatenate([gather_ref[start : start + count, :], gather_ref[total + start : total + start + count, :]])
@@ -308,17 +334,10 @@
     width = 2 * windows * LANES
     data = jnp.concatenate(spectra(tm, core, raw_blocks, fir_taps), axis=0)
     data = data.transpose(1, 0, 2).reshape(rows, width)
-    marks = jnp.concatenate(marks)
-
-    def is_marked(words, ids):
-        word = words.reshape(-1)[(ids // LANES // 32) * LANES + ids % LANES]
-        return (word >> (ids // LANES % 32)) & 1
-
-    mine = by_block[me[0]]
-    want = jnp.stack([is_marked(marks[order.index(k)], mine) for k in range(n)])
-    place = jnp.where(want > 0, jnp.cumsum(want, axis=1) - 1, -1)
-    held = is_marked(marks[0], by_block)
-    rank = jnp.cumsum(held, axis=1) - 1
+    tables = [jax.ShapeDtypeStruct((n, rows), I32)] * 2
+    place, rank = call(functools.partial(tables_kernel, n), tables)(me, *marks, by_block)
+    place = jnp.stack([place[order.index(k)] for k in range(n)])
+    held = jnp.where(rank < 0, 0, 1)
     relative = jnp.arange(n, dtype=I32) ^ me[0]
     counts = jnp.sum(held, axis=1)[relative]
     offsets = jnp.cumsum(counts) - counts
@@ -403,17 +422,17 @@
         here = [new] if i else [new, own]
         marks.append(new)
         owners = known[i] if i else known[i] + [0]
-        kernel = functools.partial(pack_kernel, list(range(len(owners))), len(here))
-        packed = call(kernel, [shaped((chunk, width), BF16)] * len(owners))(me, *here, by_block, keep, other)
+        kernel = functools.partial(pack_kernel, list(range(len(owners))), len(here), chunk)
+        packed = call(kernel, [shaped(folded(chunk, width), BF16)] * len(owners))(me, *here, by_block, keep, other)
         for k, value in zip(owners, packed):
             arrived[k] = swap(value, "chan", n, k) if k else value
 
-    shapes = [shaped((2 * pair_count, half * chunk), BF16)] * 2 + [shaped((1, 1), I32)]
+    shapes = [shaped((2 * pair_count, half * padded(chunk)), BF16)] * 2 + [shaped((1, 1), I32)]
     kernel = functools.partial(arrival_kernel, early + late, chunk, len(marks))
     pick_early, pick_late, most = call(kernel, shapes)(me, *marks, by_block, pairs.T)
-    scratch = [pltpu.VMEM((half * chunk, width), BF16)]
+    scratch = [pltpu.VMEM((half * padded(chunk), width), BF16)]
     found = call(
-        functools.partial(early_kernel, half),
+        functools.partial(early_kernel, half, chunk),
         shaped((2 * pair_count, width), BF16),
         flops=4 * pair_count * half * chunk * width,
         scratch=scratch,
@@ -424,7 +443,7 @@
     totals, seconds = [], []
     for i, size in enumerate(sizes):
         total = call(
-            functools.partial(product_kernel, half, sum(sizes[:i])),
+            functools.partial(product_kernel, half, chunk, sum(sizes[:i])),
             shaped((size, LANES), BF16),
             flops=4 * size * half * chunk * width,
             scratch=scratch,

time: 50 us -> 50.2 us (level)
  transfers between devices with their start and end apart: 15 -> 15, of which waited for: 9 -> 8; matrix products, arithmetic and copies ran while one was open for 0% -> 0% of each run, Pallas kernels for 8% -> 8%
where the time goes in v3:
time: 50.2 us; the launch traced here: 50.1 us
  starting transfers between devices  22.1 us (44%)
  waiting for transfers between devices  14.5 us (29%)
  Pallas kernels  10 us (20%)
  local copies, waits for them, and re-layouts  2.65 us (5%)
  between operations  0.76 us (2%)
    ppermute x15, starting transfers between devices, swap(): return lax.ppermute(value, axis, [(i, i ^ bit) for i in range(size)])  22.1 us
    ppermute x15, waiting for transfers between devices, swap(): return lax.ppermute(value, axis, [(i, i ^ bit) for i in range(size)])  14.5 us
    pallas_call x10, Pallas kernels, run(): pl.pallas_call(kernel, out_shape=tuple(out) if many else out, in_specs=sp...  6.67 us
    pallas_call x1, Pallas kernels, spectra(): pl.pallas_call(spectrum_kernel, out_shape=(half, half), in_specs=[SMEM, V...  3.34 us
    unnamed x10, local copies, waits for them, and re-layouts  2.64 us
  transfers between devices with their start and end apart: 15, of which 8 were waited for; matrix products, arithmetic and copies ran while one was open for 0% of the time, Pallas kernels for 8%

profile of v3, /device:TPU:0, one launch (start us, length us, event | category | flops | bytes accessed | tf_op | source)
XLA Modules:
  0.0 50.1 jit_solution(6170037488380370569)
XLA Ops:
  0.1 1.0 %copy-done.1 = bf16[1152,256]{1,0:T(8,128)(2,1)S(1)} copy-done((bf16[1152,256]{1,0:T(8,128)(2,1)S(1)}, bf16[1152,256]{1,0:T(8,128)(2,1)}, u32[]{:S(2)}) %copy-start.1) | copy-done | bytes 589848
  1.1 1.6 %copy-done.2 = bf16[4,640,1024]{2,1,0:T(8,128)(2,1)S(1)} copy-done((bf16[4,640,1024]{2,1,0:T(8,128)(2,1)S(1)}, bf16[4,640,1024]{2,1,0:T(8,128)(2,1)}, u32[]{:S(2)}) %copy-start.2) | copy-done | bytes 5242904
  2.7 3.3 %shard_map.67 = (bf16[4,640,128]{2,1,0:T(8,128)(2,1)S(1)}, bf16[4,640,128]{2,1,0:T(8,128)(2,1)S(1)}) custom-call(s32[1]{0:T(128)} %bitcast.3.core_ref, bf16[1,128]{1,0:T(2,128)(2,1)S(1)} %bitcast.38, bf16[1152,256]{1,0:T(8,128)(2,1)S(1)} %copy-done.1, bf16[256,256]{1,0:T(8,128)(2,1)S(1)} %shard_map.66.sum_ref, bf16[4,640,1024]{2,1,0:T(8,128)(2,1)S(1)} %copy-done.2), custom_call_target="tpu_custom_call" | custom-call | flops 1342177280 | bytes 5242880 | tf_op jit(solution)/shard_map/pallas_call | solution.py:313
  6.6 3.7 %collective-permute-start.10 = (s32[2,512]{1,0:T(2,128)S(1)}, s32[2,512]{1,0:T(2,128)S(1)}, u32[]{:S(2)}, u32[]{:S(2)}) collective-permute-start(s32[2,512]{1,0:T(2,128)S(1)} %bitcast.33), channel_id=1, source_target_pairs={{0,4},{1,5},{2,6},{3,7},{4,0},{5,1},{6,2},{7,3},{8,12},{9,13},{10,... | collective-permute-start | bytes 12296 | tf_op jit(solution)/shard_map/ppermute | solution.py:285
  10.3 1.6 %collective-permute-done.10.refs_1_ = s32[2,512]{1,0:T(2,128)S(1)} collective-permute-done((s32[2,512]{1,0:T(2,128)S(1)}, s32[2,512]{1,0:T(2,128)S(1)}, u32[]{:S(2)}, u32[]{:S(2)}) %collective-permute-start.10) | collective-permute-done | bytes 4128 | tf_op jit(solution)/shard_map/ppermute | solution.py:285
  12.2 1.9 %collective-permute-start.11 = (s32[2,256]{1,0:T(2,128)S(1)}, s32[2,256]{1,0:T(2,128)S(1)}, u32[]{:S(2)}, u32[]{:S(2)}) collective-permute-start(s32[2,256]{1,0:T(2,128)S(1)} %pad_add_fusion.1), channel_id=1, source_target_pairs={{0,1},{1,0},{2,3},{3,2},{4,5},{5,4},{6,7},{7,6},{8,9},{9,8},{10,11... | collective-permute-start | bytes 6152 | tf_op jit(solution)/shard_map/ppermute | solution.py:285
  14.1 1.7 %collective-permute-done.11.refs_2_.refs_0_ = s32[2,256]{1,0:T(2,128)S(1)} collective-permute-done((s32[2,256]{1,0:T(2,128)S(1)}, s32[2,256]{1,0:T(2,128)S(1)}, u32[]{:S(2)}, u32[]{:S(2)}) %collective-permute-start.11) | collective-permute-done | bytes 2080 | tf_op jit(solution)/shard_map/ppermute | solution.py:285
  16.4 1.9 %collective-permute-start.15 = (bf16[104,512]{1,0:T(8,128)(2,1)S(1)}, bf16[104,512]{1,0:T(8,128)(2,1)S(1)}, u32[]{:S(2)}, u32[]{:S(2)}) collective-permute-start(bf16[104,512]{1,0:T(8,128)(2,1)S(1)} %get-tuple-element.156), channel_id=1, source_target_pairs={{0,1},{1,0},{2,3},{3,2},{4,5},{5,4},{6,7},{7,6},{8,9},{9,8},{10,11... | collective-permute-start | bytes 319496 | tf_op jit(solution)/shard_map/ppermute | solution.py:285
  18.3 2.5 %collective-permute-start.16 = (bf16[104,512]{1,0:T(8,128)(2,1)S(1)}, bf16[104,512]{1,0:T(8,128)(2,1)S(1)}, u32[]{:S(2)}, u32[]{:S(2)}) collective-permute-start(bf16[104,512]{1,0:T(8,128)(2,1)S(1)} %get-tuple-element.157), channel_id=1, source_target_pairs={{0,5},{1,4},{2,7},{3,6},{4,1},{5,0},{6,3},{7,2},{8,13},{9,12},{10,... | collective-permute-start | bytes 319496 | tf_op jit(solution)/shard_map/ppermute | solution.py:285
  21.5 1.9 %collective-permute-start.12 = (s32[4,256]{1,0:T(4,128)S(1)}, s32[4,256]{1,0:T(4,128)S(1)}, u32[]{:S(2)}, u32[]{:S(2)}) collective-permute-start(s32[4,256]{1,0:T(4,128)S(1)} %pad_add_fusion), channel_id=1, source_target_pairs={{0,2},{1,3},{2,0},{3,1},{4,6},{5,7},{6,4},{7,5},{8,10},{9,11},{10,... | collective-permute-start | bytes 12296 | tf_op jit(solution)/shard_map/ppermute | solution.py:285
  23.4 1.8 %collective-permute-done.12.refs_3_.refs_0_ = s32[4,256]{1,0:T(4,128)S(1)} collective-permute-done((s32[4,256]{1,0:T(4,128)S(1)}, s32[4,256]{1,0:T(4,128)S(1)}, u32[]{:S(2)}, u32[]{:S(2)}) %collective-permute-start.12) | collective-permute-done | bytes 4128 | tf_op jit(solution)/shard_map/ppermute | solution.py:285
  25.2 0.7 %shard_map.71 = (bf16[104,512]{1,0:T(8,128)(2,1)S(1)}, bf16[104,512]{1,0:T(8,128)(2,1)S(1)}, bf16[104,512]{1,0:T(8,128)(2,1)S(1)}, bf16[104,512]{1,0:T(8,128)(2,1)S(1)}) custom-call(s32[1]{0:T(128)} %bitcast.me_ref, s32[4,256]{1,0:T(4,128)S(1)} %collective-permute-done.12.refs_3_.refs_0_, s32[8,640]{1,0:T(8,128)S(1)} %reshape.128.refs_4_.refs_2_.refs_1_, ...), custom_call_target="tpu_custom_call" | custom-call | bytes 1761284 | tf_op jit(solution)/shard_map/pallas_call | solution.py:294
  25.9 1.9 %collective-permute-start.17 = (bf16[104,512]{1,0:T(8,128)(2,1)S(1)}, bf16[104,512]{1,0:T(8,128)(2,1)S(1)}, u32[]{:S(2)}, u32[]{:S(2)}) collective-permute-start(bf16[104,512]{1,0:T(8,128)(2,1)S(1)} %get-tuple-element.159), channel_id=1, source_target_pairs={{0,2},{1,3},{2,0},{3,1},{4,6},{5,7},{6,4},{7,5},{8,10},{9,11},{10,... | collective-permute-start | bytes 319496 | tf_op jit(solution)/shard_map/ppermute | solution.py:285
  27.7 1.5 %collective-permute-start.18 = (bf16[104,512]{1,0:T(8,128)(2,1)S(1)}, bf16[104,512]{1,0:T(8,128)(2,1)S(1)}, u32[]{:S(2)}, u32[]{:S(2)}) collective-permute-start(bf16[104,512]{1,0:T(8,128)(2,1)S(1)} %get-tuple-element.160), channel_id=1, source_target_pairs={{0,3},{1,2},{2,1},{3,0},{4,7},{5,6},{6,5},{7,4},{8,11},{9,10},{10,... | collective-permute-start | bytes 319496 | tf_op jit(solution)/shard_map/ppermute | solution.py:285
  29.2 4.0 %collective-permute-start.19 = (bf16[104,512]{1,0:T(8,128)(2,1)S(1)}, bf16[104,512]{1,0:T(8,128)(2,1)S(1)}, u32[]{:S(2)}, u32[]{:S(2)}) collective-permute-start(bf16[104,512]{1,0:T(8,128)(2,1)S(1)} %get-tuple-element.161), channel_id=1, source_target_pairs={{0,6},{1,7},{2,4},{3,5},{4,2},{5,3},{6,0},{7,1},{8,14},{9,15},{10,... | collective-permute-start | bytes 319496 | tf_op jit(solution)/shard_map/ppermute | solution.py:285
  33.2 1.4 %shard_map.65 = (bf16[1024,224]{1,0:T(8,128)(2,1)S(1)}, bf16[1024,224]{1,0:T(8,128)(2,1)S(1)}, s32[1,1]{1,0:T(1,128)}) custom-call(s32[1]{0:T(128)} %bitcast.me_ref, s32[1,256]{1,0:T(1,128)S(1)} %get-tuple-element.437.refs_0_.refs_1_, s32[1,256]{1,0:T(1,128)S(1)} %get-tuple-element.438.refs_1_.refs_0_, s32[2,256]{1,0:T(2,128)S(1)} %collective-permute-done.11.refs_2_.refs_0_, ...), custom_call_target="tpu_custom_call" | custom-call | bytes 950280 | tf_op jit(solution)/shard_map/pallas_call | solution.py:294
  34.6 0.7 %shard_map.70.early_ref = bf16[1024,1024]{1,0:T(8,128)(2,1)S(1)} custom-call(bf16[1024,224]{1,0:T(8,128)(2,1)S(1)} %get-tuple-element.151.gather_ref, bf16[104,512]{1,0:T(8,128)(2,1)S(1)} %get-tuple-element.154.refs_0_, bf16[104,512]{1,0:T(8,128)(2,1)S(1)} %collective-permute-done.14.refs_1_, bf16[104,512]{1,0:T(8,128)(2,1)S(1)} %collective-permute-done.15.refs_2_, ...), custom_call_target="tpu_custom_call" | custom-call | flops 436207616 | bytes 2981888 | tf_op jit(solution)/shard_map/pallas_call | solution.py:294
  35.3 2.0 %collective-permute-done.19.refs_2_ = bf16[104,512]{1,0:T(8,128)(2,1)S(1)} collective-permute-done((bf16[104,512]{1,0:T(8,128)(2,1)S(1)}, bf16[104,512]{1,0:T(8,128)(2,1)S(1)}, u32[]{:S(2)}, u32[]{:S(2)}) %collective-permute-start.19) | collective-permute-done | bytes 106528 | tf_op jit(solution)/shard_map/ppermute | solution.py:285
  37.3 3.2 %collective-permute-done.20.refs_3_ = bf16[104,512]{1,0:T(8,128)(2,1)S(1)} collective-permute-done((bf16[104,512]{1,0:T(8,128)(2,1)S(1)}, bf16[104,512]{1,0:T(8,128)(2,1)S(1)}, u32[]{:S(2)}, u32[]{:S(2)}) %collective-permute-start.20) | collective-permute-done | bytes 106528 | tf_op jit(solution)/shard_map/ppermute | solution.py:285
  40.6 0.8 %shard_map.72 = bf16[320,128]{1,0:T(8,128)(2,1)S(1)} custom-call(bf16[1024,1024]{1,0:T(8,128)(2,1)S(1)} %shard_map.70.early_ref, bf16[1024,224]{1,0:T(8,128)(2,1)S(1)} %get-tuple-element.158.gather_ref, bf16[104,512]{1,0:T(8,128)(2,1)S(1)} %collective-permute-done.17.refs_0_, bf16[104,512]{1,0:T(8,128)(2,1)S(1)} %collective-permute-done.18.refs_1_, ...), custom_call_target="tpu_custom_call" | custom-call | flops 272629760 | bytes 3063808 | tf_op jit(solution)/shard_map/pallas_call | solution.py:294
  41.4 1.5 %collective-permute-start.21 = (bf16[320,128]{1,0:T(8,128)(2,1)S(1)}, bf16[320,128]{1,0:T(8,128)(2,1)S(1)}, u32[]{:S(2)}, u32[]{:S(2)}) collective-permute-start(bf16[320,128]{1,0:T(8,128)(2,1)S(1)} %shard_map.72), channel_id=1, source_target_pairs={{0,16},{8,24},{16,0},{24,8},{1,17},{9,25},{17,1},{25,9},{2,18},{10... | collective-permute-start | bytes 245768 | tf_op jit(solution)/shard_map/ppermute | solution.py:285
  44.1 1.8 %collective-permute-done.21 = bf16[320,128]{1,0:T(8,128)(2,1)S(1)} collective-permute-done((bf16[320,128]{1,0:T(8,128)(2,1)S(1)}, bf16[320,128]{1,0:T(8,128)(2,1)S(1)}, u32[]{:S(2)}, u32[]{:S(2)}) %collective-permute-start.21) | collective-permute-done | bytes 81952 | tf_op jit(solution)/shard_map/ppermute | solution.py:285
  46.0 1.7 %collective-permute-done.22 = bf16[192,128]{1,0:T(8,128)(2,1)S(1)} collective-permute-done((bf16[192,128]{1,0:T(8,128)(2,1)S(1)}, bf16[192,128]{1,0:T(8,128)(2,1)S(1)}, u32[]{:S(2)}, u32[]{:S(2)}) %collective-permute-start.22) | collective-permute-done | bytes 49184 | tf_op jit(solution)/shard_map/ppermute | solution.py:285
  49.1 1.0 %shard_map.74 = f32[512,256]{1,0:T(8,128)} custom-call(s32[1]{0:T(128)} %bitcast.3.core_ref, f32[320,128]{1,0:T(8,128)S(1)} %convert_add_fusion.refs_0_, f32[192,128]{1,0:T(8,128)S(1)} %convert_add_fusion.1.refs_1_, f32[320,128]{1,0:T(8,128)S(1)} %collective-permute-done.23.refs_2_, f32[192,128]{1,0:T(8,128)S(1)} %collective-permute-done.24.refs_3_), custom_call_target="tpu_custom_call" | custom-call | bytes 1048580 | tf_op jit(solution)/shard_map/pallas_call | solution.py:294
  (33 shorter events, 4.2 us)
Async XLA Ops:
  0.0 1.1 %copy-start.1 = (bf16[1152,256]{1,0:T(8,128)(2,1)S(1)}, bf16[1152,256]{1,0:T(8,128)(2,1)}, u32[]{:S(2)}) copy-start(bf16[1152,256]{1,0:T(8,128)(2,1)} %constant.53.clone.table_ref) | copy-start | bytes 1769476
  0.0 2.7 %copy-start.2 = (bf16[4,640,1024]{2,1,0:T(8,128)(2,1)S(1)}, bf16[4,640,1024]{2,1,0:T(8,128)(2,1)}, u32[]{:S(2)}) copy-start(bf16[4,640,1024]{2,1,0:T(8,128)(2,1)} %raw_ref.1) | copy-start | bytes 15728644
  0.0 2.7 %copy-start.17 = (bf16[128]{0:T(256)(128)(2,1)S(1)}, bf16[128]{0:T(256)(128)(2,1)}, u32[]{:S(2)}) copy-start(bf16[128]{0:T(256)(128)(2,1)} %param.11) | copy-start | bytes 772
  2.7 3.9 %copy-start.8 = (s32[512,2]{0,1:T(2,128)S(1)}, s32[512,2]{0,1:T(2,128)}, u32[]{:S(2)}) copy-start(s32[512,2]{0,1:T(2,128)} %param.13) | copy-start | bytes 12292
  2.7 11.4 %copy-start.16 = (s32[5120]{0:T(1024)S(1)}, s32[5120]{0:T(1024)}, u32[]{:S(2)}) copy-start(s32[5120]{0:T(1024)} %param.12) | copy-start | bytes 61444
  6.0 9.8 %collective-permute-start.13 = (bf16[4,640,128]{2,1,0:T(8,128)(2,1)S(1)}, bf16[4,640,128]{2,1,0:T(8,128)(2,1)S(1)}, u32[]{:S(2)}, u32[]{:S(2)}) collective-permute-start(bf16[4,640,128]{2,1,0:T(8,128)(2,1)S(1)} %get-tuple-element.153), channel_id=1, source_target_pairs={{0,8},{8,0},{16,24},{24,16},{1,9},{9,1},{17,25},{25,17},{2,10},{10... | collective-permute-start | bytes 1966088 | tf_op jit(solution)/shard_map/ppermute | solution.py:285
  6.6 5.2 %collective-permute-start.10 = (s32[2,512]{1,0:T(2,128)S(1)}, s32[2,512]{1,0:T(2,128)S(1)}, u32[]{:S(2)}, u32[]{:S(2)}) collective-permute-start(s32[2,512]{1,0:T(2,128)S(1)} %bitcast.33), channel_id=1, source_target_pairs={{0,4},{1,5},{2,6},{3,7},{4,0},{5,1},{6,2},{7,3},{8,12},{9,13},{10,... | collective-permute-start | bytes 12296 | tf_op jit(solution)/shard_map/ppermute | solution.py:285
  12.2 3.7 %collective-permute-start.11 = (s32[2,256]{1,0:T(2,128)S(1)}, s32[2,256]{1,0:T(2,128)S(1)}, u32[]{:S(2)}, u32[]{:S(2)}) collective-permute-start(s32[2,256]{1,0:T(2,128)S(1)} %pad_add_fusion.1), channel_id=1, source_target_pairs={{0,1},{1,0},{2,3},{3,2},{4,5},{5,4},{6,7},{7,6},{8,9},{9,8},{10,11... | collective-permute-start | bytes 6152 | tf_op jit(solution)/shard_map/ppermute | solution.py:285
  16.4 12.8 %collective-permute-start.15 = (bf16[104,512]{1,0:T(8,128)(2,1)S(1)}, bf16[104,512]{1,0:T(8,128)(2,1)S(1)}, u32[]{:S(2)}, u32[]{:S(2)}) collective-permute-start(bf16[104,512]{1,0:T(8,128)(2,1)S(1)} %get-tuple-element.156), channel_id=1, source_target_pairs={{0,1},{1,0},{2,3},{3,2},{4,5},{5,4},{6,7},{7,6},{8,9},{9,8},{10,11... | collective-permute-start | bytes 319496 | tf_op jit(solution)/shard_map/ppermute | solution.py:285
  18.3 14.9 %collective-permute-start.16 = (bf16[104,512]{1,0:T(8,128)(2,1)S(1)}, bf16[104,512]{1,0:T(8,128)(2,1)S(1)}, u32[]{:S(2)}, u32[]{:S(2)}) collective-permute-start(bf16[104,512]{1,0:T(8,128)(2,1)S(1)} %get-tuple-element.157), channel_id=1, source_target_pairs={{0,5},{1,4},{2,7},{3,6},{4,1},{5,0},{6,3},{7,2},{8,13},{9,12},{10,... | collective-permute-start | bytes 319496 | tf_op jit(solution)/shard_map/ppermute | solution.py:285
  21.4 13.2 %collective-permute-start.14 = (bf16[104,512]{1,0:T(8,128)(2,1)S(1)}, bf16[104,512]{1,0:T(8,128)(2,1)S(1)}, u32[]{:S(2)}, u32[]{:S(2)}) collective-permute-start(bf16[104,512]{1,0:T(8,128)(2,1)S(1)} %get-tuple-element.155), channel_id=1, source_target_pairs={{0,4},{1,5},{2,6},{3,7},{4,0},{5,1},{6,2},{7,3},{8,12},{9,13},{10,... | collective-permute-start | bytes 319496 | tf_op jit(solution)/shard_map/ppermute | solution.py:285
  21.5 3.7 %collective-permute-start.12 = (s32[4,256]{1,0:T(4,128)S(1)}, s32[4,256]{1,0:T(4,128)S(1)}, u32[]{:S(2)}, u32[]{:S(2)}) collective-permute-start(s32[4,256]{1,0:T(4,128)S(1)} %pad_add_fusion), channel_id=1, source_target_pairs={{0,2},{1,3},{2,0},{3,1},{4,6},{5,7},{6,4},{7,5},{8,10},{9,11},{10,... | collective-permute-start | bytes 12296 | tf_op jit(solution)/shard_map/ppermute | solution.py:285
  25.9 9.4 %collective-permute-start.17 = (bf16[104,512]{1,0:T(8,128)(2,1)S(1)}, bf16[104,512]{1,0:T(8,128)(2,1)S(1)}, u32[]{:S(2)}, u32[]{:S(2)}) collective-permute-start(bf16[104,512]{1,0:T(8,128)(2,1)S(1)} %get-tuple-element.159), channel_id=1, source_target_pairs={{0,2},{1,3},{2,0},{3,1},{4,6},{5,7},{6,4},{7,5},{8,10},{9,11},{10,... | collective-permute-start | bytes 319496 | tf_op jit(solution)/shard_map/ppermute | solution.py:285
  27.7 7.6 %collective-permute-start.18 = (bf16[104,512]{1,0:T(8,128)(2,1)S(1)}, bf16[104,512]{1,0:T(8,128)(2,1)S(1)}, u32[]{:S(2)}, u32[]{:S(2)}) collective-permute-start(bf16[104,512]{1,0:T(8,128)(2,1)S(1)} %get-tuple-element.160), channel_id=1, source_target_pairs={{0,3},{1,2},{2,1},{3,0},{4,7},{5,6},{6,5},{7,4},{8,11},{9,10},{10,... | collective-permute-start | bytes 319496 | tf_op jit(solution)/shard_map/ppermute | solution.py:285
  29.2 8.1 %collective-permute-start.19 = (bf16[104,512]{1,0:T(8,128)(2,1)S(1)}, bf16[104,512]{1,0:T(8,128)(2,1)S(1)}, u32[]{:S(2)}, u32[]{:S(2)}) collective-permute-start(bf16[104,512]{1,0:T(8,128)(2,1)S(1)} %get-tuple-element.161), channel_id=1, source_target_pairs={{0,6},{1,7},{2,4},{3,5},{4,2},{5,3},{6,0},{7,1},{8,14},{9,15},{10,... | collective-permute-start | bytes 319496 | tf_op jit(solution)/shard_map/ppermute | solution.py:285
  33.2 7.4 %collective-permute-start.20 = (bf16[104,512]{1,0:T(8,128)(2,1)S(1)}, bf16[104,512]{1,0:T(8,128)(2,1)S(1)}, u32[]{:S(2)}, u32[]{:S(2)}) collective-permute-start(bf16[104,512]{1,0:T(8,128)(2,1)S(1)} %get-tuple-element.162), channel_id=1, source_target_pairs={{0,7},{1,6},{2,5},{3,4},{4,3},{5,2},{6,1},{7,0},{8,15},{9,14},{10,... | collective-permute-start | bytes 319496 | tf_op jit(solution)/shard_map/ppermute | solution.py:285
  41.4 4.5 %collective-permute-start.21 = (bf16[320,128]{1,0:T(8,128)(2,1)S(1)}, bf16[320,128]{1,0:T(8,128)(2,1)S(1)}, u32[]{:S(2)}, u32[]{:S(2)}) collective-permute-start(bf16[320,128]{1,0:T(8,128)(2,1)S(1)} %shard_map.72), channel_id=1, source_target_pairs={{0,16},{8,24},{16,0},{24,8},{1,17},{9,25},{17,1},{25,9},{2,18},{10... | collective-permute-start | bytes 245768 | tf_op jit(solution)/shard_map/ppermute | solution.py:285
  43.5 4.2 %collective-permute-start.22 = (bf16[192,128]{1,0:T(8,128)(2,1)S(1)}, bf16[192,128]{1,0:T(8,128)(2,1)S(1)}, u32[]{:S(2)}, u32[]{:S(2)}) collective-permute-start(bf16[192,128]{1,0:T(8,128)(2,1)S(1)} %shard_map.73), channel_id=1, source_target_pairs={{0,16},{8,24},{16,0},{24,8},{1,17},{9,25},{17,1},{25,9},{2,18},{10... | collective-permute-start | bytes 147464 | tf_op jit(solution)/shard_map/ppermute | solution.py:285
  45.9 3.1 %collective-permute-start.23 = (f32[320,128]{1,0:T(8,128)S(1)}, f32[320,128]{1,0:T(8,128)S(1)}, u32[]{:S(2)}, u32[]{:S(2)}) collective-permute-start(f32[320,128]{1,0:T(8,128)S(1)} %convert_add_fusion.refs_0_), channel_id=1, source_target_pairs={{0,8},{8,0},{16,24},{24,16},{1,9},{9,1},{17,25},{25,17},{2,10},{10... | collective-permute-start | bytes 491528 | tf_op jit(solution)/shard_map/ppermute | solution.py:285
  47.7 1.4 %collective-permute-start.24 = (f32[192,128]{1,0:T(8,128)S(1)}, f32[192,128]{1,0:T(8,128)S(1)}, u32[]{:S(2)}, u32[]{:S(2)}) collective-permute-start(f32[192,128]{1,0:T(8,128)S(1)} %convert_add_fusion.1.refs_1_), channel_id=1, source_target_pairs={{0,8},{8,0},{16,24},{24,16},{1,9},{9,1},{17,25},{25,17},{2,10},{10... | collective-permute-start | bytes 294920 | tf_op jit(solution)/shard_map/ppermute | solution.py:285

commit v4 on v3

--- a/solution.py
+++ b/solution.py
@@ -13,7 +13,7 @@
 SMOOTH = 4
 LANES = 128
 FIRST_FLOPS = 2 * 10**10
-SENDS = [4, 1, 5, 2, 3, 6, 7]
+SENDS = [4, 1, 5, 3, 6, 2, 7]
 EARLY = [0, 4, 1, 5]
 ROUND_ROWS = 52
 
@@ -81,8 +81,8 @@
         keep_ref[w] = jnp.where(first_core, first, second).astype(BF16)
         give_ref[w] = jnp.where(first_core, second, first).astype(BF16)
 
-    for start in range(0, windows, 2):
-        pair = range(start, min(start + 2, windows))
+    for start in range(0, windows, 4):
+        pair = range(start, min(start + 4, windows))
         for w in pair:
             copies[w].wait()
         specs = [dot(rows_ref[w], mat_ref[...]) for w in pair]
@@ -439,7 +439,7 @@
         smem=0,
     )(pick_early, *[arrived[k] for k in early])
 
-    sizes = [pair_count * 5 // 8, pair_count * 3 // 8]
+    sizes = [pair_count * 3 // 4, pair_count // 4]
     totals, seconds = [], []
     for i, size in enumerate(sizes):
         total = call(

time: 50.2 us -> 49 us (0.976)
  waiting for transfers between devices: 14.5 us -> 13.5 us
    ppermute x15, waiting for transfers between devices: 14.5 us -> 13.5 us  [swap(): return lax.ppermute(value, axis, [(i, i ^ bit) for i in range(size)])]
  transfers between devices with their start and end apart: 15 -> 15, of which waited for: 8 -> 9; matrix products, arithmetic and copies ran while one was open for 0% -> 0% of each run, Pallas kernels for 8% -> 8%
where the time goes in v4:
time: 49 us; the launch traced here: 48.9 us
  starting transfers between devices  22.1 us (45%)
  waiting for transfers between devices  13.5 us (28%)
  Pallas kernels  9.81 us (20%)
  local copies, waits for them, and re-layouts  2.65 us (5%)
  between operations  0.76 us (2%)
    ppermute x15, starting transfers between devices, swap(): return lax.ppermute(value, axis, [(i, i ^ bit) for i in range(size)])  22.1 us
    ppermute x15, waiting for transfers between devices, swap(): return lax.ppermute(value, axis, [(i, i ^ bit) for i in range(size)])  13.5 us
    pallas_call x10, Pallas kernels, run(): pl.pallas_call(kernel, out_shape=tuple(out) if many else out, in_specs=sp...  6.71 us
    pallas_call x1, Pallas kernels, spectra(): pl.pallas_call(spectrum_kernel, out_shape=(half, half), in_specs=[SMEM, V...  3.1 us
    unnamed x10, local copies, waits for them, and re-layouts  2.64 us
  transfers between devices with their start and end apart: 15, of which 9 were waited for; matrix products, arithmetic and copies ran while one was open for 0% of the time, Pallas kernels for 8%

profile of v4, /device:TPU:0, one launch (start us, length us, event | category | flops | bytes accessed | tf_op | source)
XLA Modules:
  0.0 48.9 jit_solution(6262750802908341305)
XLA Ops:
  0.1 1.0 %copy-done.1 = bf16[1152,256]{1,0:T(8,128)(2,1)S(1)} copy-done((bf16[1152,256]{1,0:T(8,128)(2,1)S(1)}, bf16[1152,256]{1,0:T(8,128)(2,1)}, u32[]{:S(2)}) %copy-start.1) | copy-done | bytes 589848
  1.1 1.6 %copy-done.2 = bf16[4,640,1024]{2,1,0:T(8,128)(2,1)S(1)} copy-done((bf16[4,640,1024]{2,1,0:T(8,128)(2,1)S(1)}, bf16[4,640,1024]{2,1,0:T(8,128)(2,1)}, u32[]{:S(2)}) %copy-start.2) | copy-done | bytes 5242904
  2.7 3.1 %shard_map.67 = (bf16[4,640,128]{2,1,0:T(8,128)(2,1)S(1)}, bf16[4,640,128]{2,1,0:T(8,128)(2,1)S(1)}) custom-call(s32[1]{0:T(128)} %bitcast.3.core_ref, bf16[1,128]{1,0:T(2,128)(2,1)S(1)} %bitcast.38, bf16[1152,256]{1,0:T(8,128)(2,1)S(1)} %copy-done.1, bf16[256,256]{1,0:T(8,128)(2,1)S(1)} %shard_map.66.sum_ref, bf16[4,640,1024]{2,1,0:T(8,128)(2,1)S(1)} %copy-done.2), custom_call_target="tpu_custom_call" | custom-call | flops 1342177280 | bytes 5242880 | tf_op jit(solution)/shard_map/pallas_call | solution.py:313
  6.4 3.7 %collective-permute-start.10 = (s32[2,512]{1,0:T(2,128)S(1)}, s32[2,512]{1,0:T(2,128)S(1)}, u32[]{:S(2)}, u32[]{:S(2)}) collective-permute-start(s32[2,512]{1,0:T(2,128)S(1)} %bitcast.33), channel_id=1, source_target_pairs={{0,4},{1,5},{2,6},{3,7},{4,0},{5,1},{6,2},{7,3},{8,12},{9,13},{10,... | collective-permute-start | bytes 12296 | tf_op jit(solution)/shard_map/ppermute | solution.py:285
  10.0 1.6 %collective-permute-done.10.refs_1_ = s32[2,512]{1,0:T(2,128)S(1)} collective-permute-done((s32[2,512]{1,0:T(2,128)S(1)}, s32[2,512]{1,0:T(2,128)S(1)}, u32[]{:S(2)}, u32[]{:S(2)}) %collective-permute-start.10) | collective-permute-done | bytes 4128 | tf_op jit(solution)/shard_map/ppermute | solution.py:285
  11.9 1.9 %collective-permute-start.11 = (s32[2,256]{1,0:T(2,128)S(1)}, s32[2,256]{1,0:T(2,128)S(1)}, u32[]{:S(2)}, u32[]{:S(2)}) collective-permute-start(s32[2,256]{1,0:T(2,128)S(1)} %pad_add_fusion.1), channel_id=1, source_target_pairs={{0,1},{1,0},{2,3},{3,2},{4,5},{5,4},{6,7},{7,6},{8,9},{9,8},{10,11... | collective-permute-start | bytes 6152 | tf_op jit(solution)/shard_map/ppermute | solution.py:285
  13.8 1.7 %collective-permute-done.11.refs_2_.refs_0_ = s32[2,256]{1,0:T(2,128)S(1)} collective-permute-done((s32[2,256]{1,0:T(2,128)S(1)}, s32[2,256]{1,0:T(2,128)S(1)}, u32[]{:S(2)}, u32[]{:S(2)}) %collective-permute-start.11) | collective-permute-done | bytes 2080 | tf_op jit(solution)/shard_map/ppermute | solution.py:285
  16.1 1.9 %collective-permute-start.15 = (bf16[104,512]{1,0:T(8,128)(2,1)S(1)}, bf16[104,512]{1,0:T(8,128)(2,1)S(1)}, u32[]{:S(2)}, u32[]{:S(2)}) collective-permute-start(bf16[104,512]{1,0:T(8,128)(2,1)S(1)} %get-tuple-element.156), channel_id=1, source_target_pairs={{0,1},{1,0},{2,3},{3,2},{4,5},{5,4},{6,7},{7,6},{8,9},{9,8},{10,11... | collective-permute-start | bytes 319496 | tf_op jit(solution)/shard_map/ppermute | solution.py:285
  18.0 2.5 %collective-permute-start.16 = (bf16[104,512]{1,0:T(8,128)(2,1)S(1)}, bf16[104,512]{1,0:T(8,128)(2,1)S(1)}, u32[]{:S(2)}, u32[]{:S(2)}) collective-permute-start(bf16[104,512]{1,0:T(8,128)(2,1)S(1)} %get-tuple-element.157), channel_id=1, source_target_pairs={{0,5},{1,4},{2,7},{3,6},{4,1},{5,0},{6,3},{7,2},{8,13},{9,12},{10,... | collective-permute-start | bytes 319496 | tf_op jit(solution)/shard_map/ppermute | solution.py:285
  21.3 1.9 %collective-permute-start.12 = (s32[4,256]{1,0:T(4,128)S(1)}, s32[4,256]{1,0:T(4,128)S(1)}, u32[]{:S(2)}, u32[]{:S(2)}) collective-permute-start(s32[4,256]{1,0:T(4,128)S(1)} %pad_add_fusion), channel_id=1, source_target_pairs={{0,2},{1,3},{2,0},{3,1},{4,6},{5,7},{6,4},{7,5},{8,10},{9,11},{10,... | collective-permute-start | bytes 12296 | tf_op jit(solution)/shard_map/ppermute | solution.py:285
  23.1 1.8 %collective-permute-done.12.refs_3_.refs_0_ = s32[4,256]{1,0:T(4,128)S(1)} collective-permute-done((s32[4,256]{1,0:T(4,128)S(1)}, s32[4,256]{1,0:T(4,128)S(1)}, u32[]{:S(2)}, u32[]{:S(2)}) %collective-permute-start.12) | collective-permute-done | bytes 4128 | tf_op jit(solution)/shard_map/ppermute | solution.py:285
  25.6 2.8 %collective-permute-start.17 = (bf16[104,512]{1,0:T(8,128)(2,1)S(1)}, bf16[104,512]{1,0:T(8,128)(2,1)S(1)}, u32[]{:S(2)}, u32[]{:S(2)}) collective-permute-start(bf16[104,512]{1,0:T(8,128)(2,1)S(1)} %get-tuple-element.159), channel_id=1, source_target_pairs={{0,3},{1,2},{2,1},{3,0},{4,7},{5,6},{6,5},{7,4},{8,11},{9,10},{10,... | collective-permute-start | bytes 319496 | tf_op jit(solution)/shard_map/ppermute | solution.py:285
  28.5 3.2 %collective-permute-start.18 = (bf16[104,512]{1,0:T(8,128)(2,1)S(1)}, bf16[104,512]{1,0:T(8,128)(2,1)S(1)}, u32[]{:S(2)}, u32[]{:S(2)}) collective-permute-start(bf16[104,512]{1,0:T(8,128)(2,1)S(1)} %get-tuple-element.160), channel_id=1, source_target_pairs={{0,6},{1,7},{2,4},{3,5},{4,2},{5,3},{6,0},{7,1},{8,14},{9,15},{10,... | collective-permute-start | bytes 319496 | tf_op jit(solution)/shard_map/ppermute | solution.py:285
  32.0 0.8 %collective-permute-start.20 = (bf16[104,512]{1,0:T(8,128)(2,1)S(1)}, bf16[104,512]{1,0:T(8,128)(2,1)S(1)}, u32[]{:S(2)}, u32[]{:S(2)}) collective-permute-start(bf16[104,512]{1,0:T(8,128)(2,1)S(1)} %get-tuple-element.162), channel_id=1, source_target_pairs={{0,7},{1,6},{2,5},{3,4},{4,3},{5,2},{6,1},{7,0},{8,15},{9,14},{10,... | collective-permute-start | bytes 319496 | tf_op jit(solution)/shard_map/ppermute | solution.py:285
  32.9 1.4 %shard_map.65 = (bf16[1024,224]{1,0:T(8,128)(2,1)S(1)}, bf16[1024,224]{1,0:T(8,128)(2,1)S(1)}, s32[1,1]{1,0:T(1,128)}) custom-call(s32[1]{0:T(128)} %bitcast.me_ref, s32[1,256]{1,0:T(1,128)S(1)} %get-tuple-element.437.refs_0_.refs_1_, s32[1,256]{1,0:T(1,128)S(1)} %get-tuple-element.438.refs_1_.refs_0_, s32[2,256]{1,0:T(2,128)S(1)} %collective-permute-done.11.refs_2_.refs_0_, ...), custom_call_target="tpu_custom_call" | custom-call | bytes 950280 | tf_op jit(solution)/shard_map/pallas_call | solution.py:294
  34.3 0.7 %shard_map.70.early_ref = bf16[1024,1024]{1,0:T(8,128)(2,1)S(1)} custom-call(bf16[1024,224]{1,0:T(8,128)(2,1)S(1)} %get-tuple-element.151.gather_ref, bf16[104,512]{1,0:T(8,128)(2,1)S(1)} %get-tuple-element.154.refs_0_, bf16[104,512]{1,0:T(8,128)(2,1)S(1)} %collective-permute-done.14.refs_1_, bf16[104,512]{1,0:T(8,128)(2,1)S(1)} %collective-permute-done.15.refs_2_, ...), custom_call_target="tpu_custom_call" | custom-call | flops 436207616 | bytes 2981888 | tf_op jit(solution)/shard_map/pallas_call | solution.py:294
  35.0 1.9 %collective-permute-done.18.refs_1_ = bf16[104,512]{1,0:T(8,128)(2,1)S(1)} collective-permute-done((bf16[104,512]{1,0:T(8,128)(2,1)S(1)}, bf16[104,512]{1,0:T(8,128)(2,1)S(1)}, u32[]{:S(2)}, u32[]{:S(2)}) %collective-permute-start.18) | collective-permute-done | bytes 106528 | tf_op jit(solution)/shard_map/ppermute | solution.py:285
  36.9 0.9 %collective-permute-done.19.refs_2_ = bf16[104,512]{1,0:T(8,128)(2,1)S(1)} collective-permute-done((bf16[104,512]{1,0:T(8,128)(2,1)S(1)}, bf16[104,512]{1,0:T(8,128)(2,1)S(1)}, u32[]{:S(2)}, u32[]{:S(2)}) %collective-permute-start.19) | collective-permute-done | bytes 106528 | tf_op jit(solution)/shard_map/ppermute | solution.py:285
  37.8 1.7 %collective-permute-done.20.refs_3_ = bf16[104,512]{1,0:T(8,128)(2,1)S(1)} collective-permute-done((bf16[104,512]{1,0:T(8,128)(2,1)S(1)}, bf16[104,512]{1,0:T(8,128)(2,1)S(1)}, u32[]{:S(2)}, u32[]{:S(2)}) %collective-permute-start.20) | collective-permute-done | bytes 106528 | tf_op jit(solution)/shard_map/ppermute | solution.py:285
  39.5 1.0 %shard_map.72 = bf16[384,128]{1,0:T(8,128)(2,1)S(1)} custom-call(bf16[1024,1024]{1,0:T(8,128)(2,1)S(1)} %shard_map.70.early_ref, bf16[1024,224]{1,0:T(8,128)(2,1)S(1)} %get-tuple-element.158.gather_ref, bf16[104,512]{1,0:T(8,128)(2,1)S(1)} %collective-permute-done.17.refs_0_, bf16[104,512]{1,0:T(8,128)(2,1)S(1)} %collective-permute-done.18.refs_1_, ...), custom_call_target="tpu_custom_call" | custom-call | flops 327155712 | bytes 3080192 | tf_op jit(solution)/shard_map/pallas_call | solution.py:294
  40.5 1.5 %collective-permute-start.21 = (bf16[384,128]{1,0:T(8,128)(2,1)S(1)}, bf16[384,128]{1,0:T(8,128)(2,1)S(1)}, u32[]{:S(2)}, u32[]{:S(2)}) collective-permute-start(bf16[384,128]{1,0:T(8,128)(2,1)S(1)} %shard_map.72), channel_id=1, source_target_pairs={{0,16},{8,24},{16,0},{24,8},{1,17},{9,25},{17,1},{25,9},{2,18},{10... | collective-permute-start | bytes 294920 | tf_op jit(solution)/shard_map/ppermute | solution.py:285
  43.1 2.1 %collective-permute-done.21 = bf16[384,128]{1,0:T(8,128)(2,1)S(1)} collective-permute-done((bf16[384,128]{1,0:T(8,128)(2,1)S(1)}, bf16[384,128]{1,0:T(8,128)(2,1)S(1)}, u32[]{:S(2)}, u32[]{:S(2)}) %collective-permute-start.21) | collective-permute-done | bytes 98336 | tf_op jit(solution)/shard_map/ppermute | solution.py:285
  45.3 1.2 %collective-permute-done.22 = bf16[128,128]{1,0:T(8,128)(2,1)S(1)} collective-permute-done((bf16[128,128]{1,0:T(8,128)(2,1)S(1)}, bf16[128,128]{1,0:T(8,128)(2,1)S(1)}, u32[]{:S(2)}, u32[]{:S(2)}) %collective-permute-start.22) | collective-permute-done | bytes 32800 | tf_op jit(solution)/shard_map/ppermute | solution.py:285
  47.8 1.0 %shard_map.74 = f32[512,256]{1,0:T(8,128)} custom-call(s32[1]{0:T(128)} %bitcast.3.core_ref, f32[384,128]{1,0:T(8,128)S(1)} %convert_add_fusion.refs_0_, f32[128,128]{1,0:T(8,128)S(1)} %convert_add_fusion.1.refs_1_, f32[384,128]{1,0:T(8,128)S(1)} %collective-permute-done.23.refs_2_, f32[128,128]{1,0:T(8,128)S(1)} %collective-permute-done.24.refs_3_), custom_call_target="tpu_custom_call" | custom-call | bytes 1048580 | tf_op jit(solution)/shard_map/pallas_call | solution.py:294
  (33 shorter events, 5.1 us)
Async XLA Ops:
  0.0 1.1 %copy-start.1 = (bf16[1152,256]{1,0:T(8,128)(2,1)S(1)}, bf16[1152,256]{1,0:T(8,128)(2,1)}, u32[]{:S(2)}) copy-start(bf16[1152,256]{1,0:T(8,128)(2,1)} %constant.53.clone.table_ref) | copy-start | bytes 1769476
  0.0 2.7 %copy-start.2 = (bf16[4,640,1024]{2,1,0:T(8,128)(2,1)S(1)}, bf16[4,640,1024]{2,1,0:T(8,128)(2,1)}, u32[]{:S(2)}) copy-start(bf16[4,640,1024]{2,1,0:T(8,128)(2,1)} %raw_ref.1) | copy-start | bytes 15728644
  0.0 2.7 %copy-start.17 = (bf16[128]{0:T(256)(128)(2,1)S(1)}, bf16[128]{0:T(256)(128)(2,1)}, u32[]{:S(2)}) copy-start(bf16[128]{0:T(256)(128)(2,1)} %param.11) | copy-start | bytes 772
  2.7 3.7 %copy-start.8 = (s32[512,2]{0,1:T(2,128)S(1)}, s32[512,2]{0,1:T(2,128)}, u32[]{:S(2)}) copy-start(s32[512,2]{0,1:T(2,128)} %param.13) | copy-start | bytes 12292
  2.7 11.2 %copy-start.16 = (s32[5120]{0:T(1024)S(1)}, s32[5120]{0:T(1024)}, u32[]{:S(2)}) copy-start(s32[5120]{0:T(1024)} %param.12) | copy-start | bytes 61444
  5.8 9.8 %collective-permute-start.13 = (bf16[4,640,128]{2,1,0:T(8,128)(2,1)S(1)}, bf16[4,640,128]{2,1,0:T(8,128)(2,1)S(1)}, u32[]{:S(2)}, u32[]{:S(2)}) collective-permute-start(bf16[4,640,128]{2,1,0:T(8,128)(2,1)S(1)} %get-tuple-element.153), channel_id=1, source_target_pairs={{0,8},{8,0},{16,24},{24,16},{1,9},{9,1},{17,25},{25,17},{2,10},{10... | collective-permute-start | bytes 1966088 | tf_op jit(solution)/shard_map/ppermute | solution.py:285
  6.4 5.2 %collective-permute-start.10 = (s32[2,512]{1,0:T(2,128)S(1)}, s32[2,512]{1,0:T(2,128)S(1)}, u32[]{:S(2)}, u32[]{:S(2)}) collective-permute-start(s32[2,512]{1,0:T(2,128)S(1)} %bitcast.33), channel_id=1, source_target_pairs={{0,4},{1,5},{2,6},{3,7},{4,0},{5,1},{6,2},{7,3},{8,12},{9,13},{10,... | collective-permute-start | bytes 12296 | tf_op jit(solution)/shard_map/ppermute | solution.py:285
  11.9 3.7 %collective-permute-start.11 = (s32[2,256]{1,0:T(2,128)S(1)}, s32[2,256]{1,0:T(2,128)S(1)}, u32[]{:S(2)}, u32[]{:S(2)}) collective-permute-start(s32[2,256]{1,0:T(2,128)S(1)} %pad_add_fusion.1), channel_id=1, source_target_pairs={{0,1},{1,0},{2,3},{3,2},{4,5},{5,4},{6,7},{7,6},{8,9},{9,8},{10,11... | collective-permute-start | bytes 6152 | tf_op jit(solution)/shard_map/ppermute | solution.py:285
  16.1 15.6 %collective-permute-start.15 = (bf16[104,512]{1,0:T(8,128)(2,1)S(1)}, bf16[104,512]{1,0:T(8,128)(2,1)S(1)}, u32[]{:S(2)}, u32[]{:S(2)}) collective-permute-start(bf16[104,512]{1,0:T(8,128)(2,1)S(1)} %get-tuple-element.156), channel_id=1, source_target_pairs={{0,1},{1,0},{2,3},{3,2},{4,5},{5,4},{6,7},{7,6},{8,9},{9,8},{10,11... | collective-permute-start | bytes 319496 | tf_op jit(solution)/shard_map/ppermute | solution.py:285
  18.0 14.0 %collective-permute-start.16 = (bf16[104,512]{1,0:T(8,128)(2,1)S(1)}, bf16[104,512]{1,0:T(8,128)(2,1)S(1)}, u32[]{:S(2)}, u32[]{:S(2)}) collective-permute-start(bf16[104,512]{1,0:T(8,128)(2,1)S(1)} %get-tuple-element.157), channel_id=1, source_target_pairs={{0,5},{1,4},{2,7},{3,6},{4,1},{5,0},{6,3},{7,2},{8,13},{9,12},{10,... | collective-permute-start | bytes 319496 | tf_op jit(solution)/shard_map/ppermute | solution.py:285
  21.1 13.1 %collective-permute-start.14 = (bf16[104,512]{1,0:T(8,128)(2,1)S(1)}, bf16[104,512]{1,0:T(8,128)(2,1)S(1)}, u32[]{:S(2)}, u32[]{:S(2)}) collective-permute-start(bf16[104,512]{1,0:T(8,128)(2,1)S(1)} %get-tuple-element.155), channel_id=1, source_target_pairs={{0,4},{1,5},{2,6},{3,7},{4,0},{5,1},{6,2},{7,3},{8,12},{9,13},{10,... | collective-permute-start | bytes 319496 | tf_op jit(solution)/shard_map/ppermute | solution.py:285
  21.3 3.7 %collective-permute-start.12 = (s32[4,256]{1,0:T(4,128)S(1)}, s32[4,256]{1,0:T(4,128)S(1)}, u32[]{:S(2)}, u32[]{:S(2)}) collective-permute-start(s32[4,256]{1,0:T(4,128)S(1)} %pad_add_fusion), channel_id=1, source_target_pairs={{0,2},{1,3},{2,0},{3,1},{4,6},{5,7},{6,4},{7,5},{8,10},{9,11},{10,... | collective-permute-start | bytes 12296 | tf_op jit(solution)/shard_map/ppermute | solution.py:285
  25.6 9.4 %collective-permute-start.17 = (bf16[104,512]{1,0:T(8,128)(2,1)S(1)}, bf16[104,512]{1,0:T(8,128)(2,1)S(1)}, u32[]{:S(2)}, u32[]{:S(2)}) collective-permute-start(bf16[104,512]{1,0:T(8,128)(2,1)S(1)} %get-tuple-element.159), channel_id=1, source_target_pairs={{0,3},{1,2},{2,1},{3,0},{4,7},{5,6},{6,5},{7,4},{8,11},{9,10},{10,... | collective-permute-start | bytes 319496 | tf_op jit(solution)/shard_map/ppermute | solution.py:285
  28.5 8.4 %collective-permute-start.18 = (bf16[104,512]{1,0:T(8,128)(2,1)S(1)}, bf16[104,512]{1,0:T(8,128)(2,1)S(1)}, u32[]{:S(2)}, u32[]{:S(2)}) collective-permute-start(bf16[104,512]{1,0:T(8,128)(2,1)S(1)} %get-tuple-element.160), channel_id=1, source_target_pairs={{0,6},{1,7},{2,4},{3,5},{4,2},{5,3},{6,0},{7,1},{8,14},{9,15},{10,... | collective-permute-start | bytes 319496 | tf_op jit(solution)/shard_map/ppermute | solution.py:285
  31.7 6.1 %collective-permute-start.19 = (bf16[104,512]{1,0:T(8,128)(2,1)S(1)}, bf16[104,512]{1,0:T(8,128)(2,1)S(1)}, u32[]{:S(2)}, u32[]{:S(2)}) collective-permute-start(bf16[104,512]{1,0:T(8,128)(2,1)S(1)} %get-tuple-element.161), channel_id=1, source_target_pairs={{0,2},{1,3},{2,0},{3,1},{4,6},{5,7},{6,4},{7,5},{8,10},{9,11},{10,... | collective-permute-start | bytes 319496 | tf_op jit(solution)/shard_map/ppermute | solution.py:285
  32.0 7.5 %collective-permute-start.20 = (bf16[104,512]{1,0:T(8,128)(2,1)S(1)}, bf16[104,512]{1,0:T(8,128)(2,1)S(1)}, u32[]{:S(2)}, u32[]{:S(2)}) collective-permute-start(bf16[104,512]{1,0:T(8,128)(2,1)S(1)} %get-tuple-element.162), channel_id=1, source_target_pairs={{0,7},{1,6},{2,5},{3,4},{4,3},{5,2},{6,1},{7,0},{8,15},{9,14},{10,... | collective-permute-start | bytes 319496 | tf_op jit(solution)/shard_map/ppermute | solution.py:285
  40.5 4.7 %collective-permute-start.21 = (bf16[384,128]{1,0:T(8,128)(2,1)S(1)}, bf16[384,128]{1,0:T(8,128)(2,1)S(1)}, u32[]{:S(2)}, u32[]{:S(2)}) collective-permute-start(bf16[384,128]{1,0:T(8,128)(2,1)S(1)} %shard_map.72), channel_id=1, source_target_pairs={{0,16},{8,24},{16,0},{24,8},{1,17},{9,25},{17,1},{25,9},{2,18},{10... | collective-permute-start | bytes 294920 | tf_op jit(solution)/shard_map/ppermute | solution.py:285
  42.5 4.0 %collective-permute-start.22 = (bf16[128,128]{1,0:T(8,128)(2,1)S(1)}, bf16[128,128]{1,0:T(8,128)(2,1)S(1)}, u32[]{:S(2)}, u32[]{:S(2)}) collective-permute-start(bf16[128,128]{1,0:T(8,128)(2,1)S(1)} %shard_map.73), channel_id=1, source_target_pairs={{0,16},{8,24},{16,0},{24,8},{1,17},{9,25},{17,1},{25,9},{2,18},{10... | collective-permute-start | bytes 98312 | tf_op jit(solution)/shard_map/ppermute | solution.py:285
  45.2 2.6 %collective-permute-start.23 = (f32[384,128]{1,0:T(8,128)S(1)}, f32[384,128]{1,0:T(8,128)S(1)}, u32[]{:S(2)}, u32[]{:S(2)}) collective-permute-start(f32[384,128]{1,0:T(8,128)S(1)} %convert_add_fusion.refs_0_), channel_id=1, source_target_pairs={{0,8},{8,0},{16,24},{24,16},{1,9},{9,1},{17,25},{25,17},{2,10},{10... | collective-permute-start | bytes 589832 | tf_op jit(solution)/shard_map/ppermute | solution.py:285
  46.5 1.3 %collective-permute-start.24 = (f32[128,128]{1,0:T(8,128)S(1)}, f32[128,128]{1,0:T(8,128)S(1)}, u32[]{:S(2)}, u32[]{:S(2)}) collective-permute-start(f32[128,128]{1,0:T(8,128)S(1)} %convert_add_fusion.1.refs_1_), channel_id=1, source_target_pairs={{0,8},{8,0},{16,24},{24,16},{1,9},{9,1},{17,25},{25,17},{2,10},{10... | collective-permute-start | bytes 196616 | tf_op jit(solution)/shard_map/ppermute | solution.py:285
